TPU v7x, 512 devices: a whole 4x4x16 slice. The times are simulated.
512 devices in a mesh: labels: 128 (over y, z, core), heads: 4 (over x).
Axes of the slice: x: 4, y: 4, z: 16, core: 2. Of those that a mesh axis runs over, the one named last changes fastest.
Arguments:
- hidden_in: bfloat16 [65536, 768], P('labels', 'heads'), may hold values from -6 to 6
- w_up: bfloat16 [768, 3072], P(None, 'heads'), may hold values from -0.21875 to 0.21875
- w_down: bfloat16 [3072, 768], P('heads'), may hold values from -0.109375 to 0.109375
- norm_gain: float32 [768], replicated, may hold values from 0.25 to 1.75
- title_length: int32 [4096], P('labels'), may hold values from 1 to 16
- label_leaf: int32 [4096], P('labels'), may hold values from 0 to 1023, as said below
- leaf_parent: int32 [1024], P('labels'), may hold values from 0 to 255
Outputs:
- label_embed: bfloat16 [4096, 768], P('labels')
- leaf_centers: float32 [1024, 768], P('labels', 'heads')
- parent_sums: float32 [256, 768], P('labels', 'heads')
Inputs may be any that keep to these rules, and one draw needn't show every extreme that they name: `label_leaf`: leaf l belongs to owner l // 8. The 32 labels of one device (an aligned block of 32 labels) name leaves of any one owner at most 2 times; in every draw one owner is named exactly 2 times by every device.
All inputs are finite; a program needn't handle non-finite values.
Results may differ from a plain program's by a relative error of at most 0.009.
Values may be sent and summed in bfloat16 or wider, within the bound.
A program may use at most 64 MiB of HBM per device.

v0:
```python
import jax
import jax.numpy as jnp
from jax import lax
from jax.sharding import Mesh
from jax.sharding import PartitionSpec as P

PAR_DEV = 2
LABELS = ("labels_0", "labels_1", "labels_2")


def copy_for_each(shard, axis):
    copies = jnp.broadcast_to(shard, (lax.axis_size(axis), *shard.shape))
    return lax.all_to_all(copies, axis, split_axis=0, concat_axis=0, tiled=True)


def in_order(parts, dim):
    parts = jnp.moveaxis(parts, 0, dim)
    shape = parts.shape
    return parts.reshape(*shape[:dim], shape[dim] * shape[dim + 1], *shape[dim + 2 :])


def gathered_copies(shard, axis, dim):
    parts = copy_for_each(shard, axis)
    return in_order(parts, dim)


def in_blocks(shard, dim, size):
    shape = shard.shape
    parts = shard.reshape(*shape[:dim], size, shape[dim] // size, *shape[dim + 1 :])
    return jnp.moveaxis(parts, dim, 0)


def sent_and_summed(shard, axis, dim):
    size = lax.axis_size(axis)
    parts = lax.all_to_all(in_blocks(shard, dim, size), axis, 0, 0, tiled=True)
    return jnp.sum(parts.astype(jnp.float32), axis=0)


def over_copies(shard, axis):
    return copy_for_each(shard, axis).sum(axis=0)


def sum_at_owner(shard, axis, dim):
    size = lax.axis_size(axis)
    parts = lax.all_to_all(in_blocks(shard, dim, size), axis, 0, 0, tiled=True)
    return jnp.sum(parts, axis=0)


def summed_rows(shard, axes, dim):
    far, near = axes
    own = sum_at_owner(in_blocks(shard, dim, lax.axis_size(far)), near, dim + 1)
    return jnp.sum(lax.all_to_all(own, far, 0, 0, tiled=True), axis=0)


def pool_rows(normed, title_length, labels_here, seq_positions):
    grouped = normed.reshape(labels_here, seq_positions, normed.shape[1])
    keep_mask = (jnp.arange(seq_positions)[None, :] < title_length[:, None]).astype(jnp.float32)
    return (
        jnp.sum(grouped * keep_mask[:, :, None], axis=1) / title_length.astype(jnp.float32)[:, None]
    )


def local(hidden_in, w_up, w_down, norm_gain, title_length, label_leaf, leaf_parent):
    token_rows = hidden_in.shape[0]
    share_cols = hidden_in.shape[1]
    full_width = w_down.shape[1]
    labels_here = label_leaf.shape[0]
    seq_positions = token_rows // labels_here
    leaf_count = leaf_parent.shape[0]
    head_index = lax.axis_index("heads")
    upward = jnp.dot(
        gathered_copies(hidden_in, "heads", 1), w_up, preferred_element_type=jnp.float32
    )
    activ = jax.nn.gelu(upward, approximate=False).astype(jnp.bfloat16)
    partial_term = (
        jnp.dot(activ, w_down, preferred_element_type=jnp.float32)
        .astype(jnp.bfloat16)
        .astype(jnp.float32)
    )
    summed = sent_and_summed(partial_term.astype(jnp.bfloat16), "heads", 1)
    mixed_share = (hidden_in.astype(jnp.float32) + summed).astype(jnp.bfloat16)
    mixed = gathered_copies(mixed_share, "heads", 1)
    as_float = mixed.astype(jnp.float32)
    mean_value = jnp.mean(as_float, axis=1, keepdims=True)
    centred = as_float - mean_value
    variance = jnp.mean(centred * centred, axis=1, keepdims=True)
    normed = centred * lax.rsqrt(variance + 1e-05) * norm_gain[None, :]
    pooled = pool_rows(normed, title_length, labels_here, seq_positions)
    scale_inv = lax.rsqrt(jnp.mean(pooled * pooled, axis=1, keepdims=True) + 1e-05)
    label_embed = (pooled * scale_inv).astype(jnp.bfloat16)
    my_columns = lax.dynamic_slice_in_dim(label_embed, head_index * share_cols, share_cols, 1)
    owner_total = lax.axis_size(LABELS)
    capacity = max(2, 2 * labels_here // owner_total)
    owner_of = label_leaf // leaf_count
    local_leaf = label_leaf - owner_of * leaf_count
    label_order = jnp.arange(labels_here)
    earlier = (owner_of[None, :] == owner_of[:, None]) & (
        label_order[None, :] < label_order[:, None]
    )
    slot_rank = jnp.sum(earlier.astype(jnp.int32), axis=1)
    target_slot = owner_of * capacity + slot_rank
    slot_ids = jnp.arange(owner_total * capacity)
    placing = slot_ids[:, None] == target_slot[None, :]
    outgoing = jnp.dot(placing.astype(jnp.bfloat16), my_columns, preferred_element_type=jnp.float32)
    outgoing = outgoing.astype(jnp.bfloat16).reshape(owner_total, capacity, share_cols)
    slot_leaf = jnp.sum(placing.astype(jnp.int32) * (local_leaf + 1)[None, :], axis=1) - 1
    slot_leaf = slot_leaf.reshape(owner_total, capacity)
    arrived, arrived_leaf = (
        lax.all_to_all(outgoing, LABELS, split_axis=0, concat_axis=0, tiled=True),
        lax.all_to_all(slot_leaf, LABELS, split_axis=0, concat_axis=0, tiled=True),
    )
    picker = (jnp.arange(leaf_count)[:, None] == arrived_leaf.reshape(1, -1)).astype(jnp.bfloat16)
    leaf_sum = jnp.dot(picker, arrived.reshape(-1, share_cols), preferred_element_type=jnp.float32)
    squares = over_copies(jnp.sum(leaf_sum * leaf_sum, axis=1), "heads")
    leaf_centers = leaf_sum * lax.rsqrt(squares / full_width + 1e-05)[:, None]
    wanted = jnp.arange(PAR_DEV * lax.axis_size(LABELS))
    picker = (wanted[:, None] == leaf_parent[None, :]).astype(jnp.float32)
    parent_sums = summed_rows(
        jnp.dot(
            picker,
            leaf_centers,
            preferred_element_type=jnp.float32,
            precision=lax.Precision.HIGHEST,
        ),
        (("labels_0", "labels_1"), "labels_2"),
        0,
    )
    return (label_embed, leaf_centers, parent_sums)


def solution(mesh):
    split = Mesh(
        mesh.devices.reshape(4, 16, 2, mesh.shape["heads"]),
        ("labels_0", "labels_1", "labels_2", "heads"),
    )
    placed = (
        P(LABELS, "heads"),
        P(None, "heads"),
        P("heads", None),
        P(),
        P(LABELS),
        P(LABELS),
        P(LABELS),
    )
    return jax.shard_map(
        local,
        mesh=split,
        in_specs=placed,
        out_specs=(P(LABELS, None), P(LABELS, "heads"), P(LABELS, "heads")),
        check_vma=False,
    )
```

profile of v0, /device:TPU:1, one launch (start us, length us, event | category | flops | bytes accessed | tf_op | source)
XLA Modules:
  0.0 152.5 jit_solution(15112835091121270142)
XLA Ops:
  0.6 0.0 copy-start
  0.6 1.1 broadcast_in_dim.6
  1.7 13.0 %all_to_all.42 = bf16[4,512,192]{1,2,0:T(8,128)(2,1)S(1)} all-to-all(bf16[4,512,192]{1,2,0:T(8,128)(2,1)S(1)} %broadcast_in_dim.6), channel_id=1, replica_groups=mesh['labels_0'=4,'labels_1'=16,'labels_2'=2,'heads'=4] {'heads'}, dimensions={0} | all-to-all | bytes 1572864 | tf_op jit(solution)/shard_map/all_to_all | solution.py:13
  14.7 6.1 %convolution_convert_fusion = bf16[512,768]{1,0:T(8,128)(2,1)S(1)} fusion(bf16[768,768]{1,0:T(8,128)(2,1)S(1)} %copy-done, bf16[512,768]{0,1:T(8,128)(2,1)S(1)} %bitcast.17, bf16[768,768]{1,0:T(8,128)(2,1)} %param.8), kind=kOutput, calls=%fused_computation.26 | convolution fusion | flops 1233911808 | bytes 3932160 | tf_op jit(solution)/shard_map/dot_general | solution.py:76
  20.8 0.0 copy-start.7
  20.9 1.2 copy.28
  22.0 3.6 %all-to-all-start.1 = ((bf16[4,512,192]{1,2,0:T(8,128)(2,1)}), bf16[4,512,192]{1,2,0:T(8,128)(2,1)S(1)}, u32[]{:S(2)}, u32[]{:S(2)}) async-start(bf16[4,512,192]{1,2,0:T(8,128)(2,1)} %bitcast.3), calls=%async_computation.1 | async-start | bytes 1572864 | tf_op jit(solution)/shard_map/all_to_all | solution.py:35
  25.7 0.2 convert_reduce_fusion.2
  25.8 8.1 %all-to-all-done.1 = bf16[4,512,192]{1,2,0:T(8,128)(2,1)S(1)} async-done(((bf16[4,512,192]{1,2,0:T(8,128)(2,1)}), bf16[4,512,192]{1,2,0:T(8,128)(2,1)S(1)}, u32[]{:S(2)}, u32[]{:S(2)}) %all-to-all-start.1) | async-done | bytes 786464 | tf_op jit(solution)/shard_map/all_to_all | solution.py:35
  33.9 0.1 convert_reduce_fusion.1
  34.1 0.0 copy-start.6
  34.1 0.9 broadcast_in_dim.7
  35.1 3.5 %all-to-all-start.2 = ((bf16[4,512,192]{1,2,0:T(8,128)(2,1)}), bf16[4,512,192]{1,2,0:T(8,128)(2,1)S(1)}, u32[]{:S(2)}, u32[]{:S(2)}) async-start(bf16[4,512,192]{1,2,0:T(8,128)(2,1)} %broadcast_in_dim.7), calls=%async_computation.2 | async-start | bytes 1572864 | tf_op jit(solution)/shard_map/all_to_all | solution.py:13
  38.6 0.1 select_reduce_fusion
  38.7 0.8 sub.37
  39.5 0.1 fusion.46
  39.5 7.3 %all-to-all-done.2 = bf16[4,512,192]{1,2,0:T(8,128)(2,1)S(1)} async-done(((bf16[4,512,192]{1,2,0:T(8,128)(2,1)}), bf16[4,512,192]{1,2,0:T(8,128)(2,1)S(1)}, u32[]{:S(2)}, u32[]{:S(2)}) %all-to-all-start.2) | async-done | bytes 786464 | tf_op jit(solution)/shard_map/all_to_all | solution.py:13
  46.9 29.0 %all-to-all-start.3 = ((s32[128,1,2]{2,1,0:T(1,128)}), s32[128,1,2]{2,1,0:T(1,128)S(1)}, u32[]{:S(2)}, u32[]{:S(2)}) async-start(s32[128,1,2]{2,1,0:T(1,128)} %bitcast.5), calls=%async_computation.3 | async-start | bytes 131072 | tf_op jit(solution)/shard_map/all_to_all | solution.py:110
  75.9 0.2 convert_reduce_fusion
  76.0 0.1 div.38
  76.1 0.3 fusion.4
  76.4 0.1 rsqrt.27
  76.5 1.4 convert_bitcast_fusion
  77.9 2.0 %copy.29 = f32[512,4,192]{2,1,0:T(4,128)S(1)} copy(f32[512,4,192]{0,2,1:T(8,128)} %convert_bitcast_fusion) | data formatting | bytes 3145728 | tf_op jit(solution)/shard_map/convert_element_type | solution.py:83
  79.8 2.5 %reshape.133 = f32[32,16,768]{2,1,0:T(8,128)} reshape(f32[512,4,192]{2,1,0:T(4,128)S(1)} %copy.29) | data formatting | bytes 3145728 | tf_op jit(solution)/shard_map/convert_element_type | solution.py:83
  82.4 2.0 %multiply_reduce_fusion = f32[32,768]{1,0:T(8,128)S(1)} fusion(f32[32,16,768]{2,1,0:T(8,128)} %reshape.133, f32[32,16]{1,0:T(8,128)S(1)} %fusion.46, f32[768]{0:T(1024)S(1)} %copy-done.4, f32[32,16]{1,0:T(8,128)S(1)} %rsqrt.27, f32[32,16]{1,0:T(8,128)S(1)} %div.38), kind=kLoop, calls=%fused_computation.9 | loop fusion | flops 1941504 | bytes 1680384 | tf_op jit(solution)/shard_map/reduce_sum | solution.py:59
  84.3 0.2 multiply_reduce_fusion.1
  84.5 0.1 multiply_convert_fusion
  84.7 0.0 copy-start.2
  84.7 0.3 convolution_convert_fusion.1
  85.0 0.1 copy.31
  85.1 0.7 reshape.131
  85.8 5.1 %all-to-all-done.3 = s32[128,1,2]{2,1,0:T(1,128)S(1)} async-done(((s32[128,1,2]{2,1,0:T(1,128)}), s32[128,1,2]{2,1,0:T(1,128)S(1)}, u32[]{:S(2)}, u32[]{:S(2)}) %all-to-all-start.3) | async-done | bytes 1056 | tf_op jit(solution)/shard_map/all_to_all | solution.py:110
  90.9 11.1 %all-to-all-start.4 = ((bf16[128,2,192]{2,1,0:T(2,128)(2,1)}), bf16[128,2,192]{2,1,0:T(2,128)(2,1)S(1)}, u32[]{:S(2)}, u32[]{:S(2)}) async-start(bf16[128,2,192]{2,1,0:T(2,128)(2,1)} %reshape.131), calls=%async_computation.4 | async-start | bytes 262144 | tf_op jit(solution)/shard_map/all_to_all | solution.py:109
  102.0 0.5 broadcast.140
  102.5 0.8 reduce.8
  103.3 0.1 eq.61
  103.5 15.8 %all-to-all-done.4 = bf16[128,2,192]{2,1,0:T(2,128)(2,1)S(1)} async-done(((bf16[128,2,192]{2,1,0:T(2,128)(2,1)}), bf16[128,2,192]{2,1,0:T(2,128)(2,1)S(1)}, u32[]{:S(2)}, u32[]{:S(2)}) %all-to-all-start.4) | async-done | bytes 98336 | tf_op jit(solution)/shard_map/all_to_all | solution.py:109
  119.3 0.1 reshape.132
  119.4 0.3 multiply_reduce_fusion.2
  119.7 6.5 %all_to_all.43 = f32[4,1,8]{2,1,0:T(1,128)S(1)} all-to-all(f32[4,1,8]{2,1,0:T(1,128)S(1)} %broadcast_in_dim.8), channel_id=1, replica_groups=mesh['labels_0'=4,'labels_1'=16,'labels_2'=2,'heads'=4] {'heads'}, dimensions={0} | all-to-all | bytes 256 | tf_op jit(solution)/shard_map/all_to_all | solution.py:13
  126.2 0.1 broadcast_multiply_fusion
  126.3 0.2 fusion.42
  126.5 0.1 reshape_reshape.3
  126.7 6.5 %all_to_all.44 = f32[2,64,2,192]{3,2,1,0:T(2,128)S(1)} all-to-all(f32[2,64,2,192]{3,2,1,0:T(2,128)S(1)} %copy.34), channel_id=1, replica_groups=mesh['labels_0'=4,'labels_1'=16,'labels_2'=2,'heads'=4] {'labels_2'}, dimensions={0} | all-to-all | bytes 393216 | tf_op jit(solution)/shard_map/all_to_all | solution.py:45
  133.3 0.2 reduce_sum.108
  133.5 18.4 %all_to_all.45 = f32[64,2,192]{2,1,0:T(2,128)S(1)} all-to-all(f32[64,2,192]{2,1,0:T(2,128)S(1)} %reduce_sum.108), channel_id=1, replica_groups=mesh['labels_0'=4,'labels_1'=16,'labels_2'=2,'heads'=4] {'labels_0','lab..., dimensions={0} | all-to-all | bytes 196608 | tf_op jit(solution)/shard_map/all_to_all | solution.py:52
  151.9 0.7 reduce_sum.109
  (24 shorter events, 0.2 us)
Async XLA Ops:
  0.6 14.1 %copy-start = (bf16[768,768]{1,0:T(8,128)(2,1)S(1)}, bf16[768,768]{1,0:T(8,128)(2,1)}, u32[]{:S(2)}) copy-start(bf16[768,768]{1,0:T(8,128)(2,1)} %param.9) | copy-start | bytes 3538948
  20.8 4.8 %copy-start.7 = (s32[32]{0:T(128)S(1)}, s32[32]{0:T(128)}, u32[]{:S(2)}) copy-start(s32[32]{0:T(128)} %param.12) | copy-start | bytes 388
  22.0 12.0 %copy-start.1 = (bf16[512,192]{0,1:T(8,128)(2,1)S(1)}, bf16[512,192]{0,1:T(8,128)(2,1)}, u32[]{:S(2)}) copy-start(bf16[512,192]{0,1:T(8,128)(2,1)} %param.7) | copy-start | bytes 589828
  22.0 11.9 %all-to-all-start.1 = ((bf16[4,512,192]{1,2,0:T(8,128)(2,1)}), bf16[4,512,192]{1,2,0:T(8,128)(2,1)S(1)}, u32[]{:S(2)}, u32[]{:S(2)}) async-start(bf16[4,512,192]{1,2,0:T(8,128)(2,1)} %bitcast.3), calls=%async_computation.1 | async-start | bytes 1572864 | tf_op jit(solution)/shard_map/all_to_all | solution.py:35
  34.1 4.5 %copy-start.6 = (s32[32]{0:T(128)S(1)}, s32[32]{0:T(128)}, u32[]{:S(2)}) copy-start(s32[32]{0:T(128)} %param.11) | copy-start | bytes 388
  35.1 11.8 %all-to-all-start.2 = ((bf16[4,512,192]{1,2,0:T(8,128)(2,1)}), bf16[4,512,192]{1,2,0:T(8,128)(2,1)S(1)}, u32[]{:S(2)}, u32[]{:S(2)}) async-start(bf16[4,512,192]{1,2,0:T(8,128)(2,1)} %broadcast_in_dim.7), calls=%async_computation.2 | async-start | bytes 1572864 | tf_op jit(solution)/shard_map/all_to_all | solution.py:13
  46.9 44.0 %all-to-all-start.3 = ((s32[128,1,2]{2,1,0:T(1,128)}), s32[128,1,2]{2,1,0:T(1,128)S(1)}, u32[]{:S(2)}, u32[]{:S(2)}) async-start(s32[128,1,2]{2,1,0:T(1,128)} %bitcast.5), calls=%async_computation.3 | async-start | bytes 131072 | tf_op jit(solution)/shard_map/all_to_all | solution.py:110
  79.8 2.5 %copy-start.4 = (f32[768]{0:T(1024)S(1)}, f32[768]{0:T(1024)}, u32[]{:S(2)}) copy-start(f32[768]{0:T(1024)} %param.10) | copy-start | bytes 9220
  82.4 43.9 %copy-start.5 = (s32[8]{0:T(128)S(1)}, s32[8]{0:T(128)}, u32[]{:S(2)}) copy-start(s32[8]{0:T(128)} %param.13) | copy-start | bytes 100
  84.7 48.6 %copy-start.2 = (bf16[32,768]{1,0:T(8,128)(2,1)}, bf16[32,768]{1,0:T(8,128)(2,1)S(1)}, u32[]{:S(2)}) copy-start(bf16[32,768]{1,0:T(8,128)(2,1)S(1)} %multiply_convert_fusion) | copy-start | bytes 147460
  90.9 28.4 %all-to-all-start.4 = ((bf16[128,2,192]{2,1,0:T(2,128)(2,1)}), bf16[128,2,192]{2,1,0:T(2,128)(2,1)S(1)}, u32[]{:S(2)}, u32[]{:S(2)}) async-start(bf16[128,2,192]{2,1,0:T(2,128)(2,1)} %reshape.131), calls=%async_computation.4 | async-start | bytes 262144 | tf_op jit(solution)/shard_map/all_to_all | solution.py:109
  126.3 26.3 %copy-start.3 = (f32[8,192]{1,0:T(8,128)}, f32[8,192]{1,0:T(8,128)S(1)}, u32[]{:S(2)}) copy-start(f32[8,192]{1,0:T(8,128)S(1)} %broadcast_multiply_fusion) | copy-start | bytes 18436
where the time goes:
time: 154 us; the launch traced here: 153 us
  starting transfers between devices  47.2 us (31%)
  blocking collectives  44.4 us (29%)
  waiting for transfers between devices  36.4 us (24%)
  local copies, waits for them, and re-layouts  10.4 us (7%)
  matrix products  6.93 us (4%)
  other arithmetic  6.37 us (4%)
    all_to_all x1, starting transfers between devices, local(): lax.all_to_all(slot_leaf, LABELS, split_axis=0, concat_axis=0, tiled=True)  29 us
    all_to_all x2, blocking collectives, copy_for_each(): return lax.all_to_all(copies, axis, split_axis=0, concat_axis=0, tiled=True)  19.4 us
    all_to_all x1, blocking collectives, summed_rows(): return jnp.sum(lax.all_to_all(own, far, 0, 0, tiled=True), axis=0)  18.4 us
    all_to_all x1, waiting for transfers between devices, local(): lax.all_to_all(outgoing, LABELS, split_axis=0, concat_axis=0, tiled=True)  15.8 us
    all_to_all x1, starting transfers between devices, local(): lax.all_to_all(outgoing, LABELS, split_axis=0, concat_axis=0, tiled=True)  11.1 us
    all_to_all x1, waiting for transfers between devices, sent_and_summed(): parts = lax.all_to_all(in_blocks(shard, dim, size), axis, 0, 0, tiled=True)  8.1 us
    all_to_all x1, waiting for transfers between devices, copy_for_each(): return lax.all_to_all(copies, axis, split_axis=0, concat_axis=0, tiled=True)  7.33 us
    all_to_all x1, blocking collectives, sum_at_owner(): parts = lax.all_to_all(in_blocks(shard, dim, size), axis, 0, 0, tiled=True)  6.54 us
  transfers between devices with their start and end apart: 4, of which 4 were waited for; matrix products, arithmetic and copies ran while one was open for 8% of the time, Pallas kernels for 0%

commit v1 on v0

v1 whole, which is shorter than its diff:
```python
import functools

import jax
import jax.numpy as jnp
from jax import lax
from jax.experimental import pallas as pl
from jax.experimental.pallas import tpu as pltpu
from jax.sharding import Mesh
from jax.sharding import PartitionSpec as P

AY, AZ, AC, AX = "labels_0", "labels_1", "labels_2", "heads"
LABELS = (AY, AZ, AC)
NX = 4
SEQ = 16
LAB = 32
LEAF = 8
PAR = 2
PIECES = 4
SHARE = 192
WIDE = 768
PAD = 256
MESH = pl.DeviceIdType.MESH
F32, BF16 = jnp.float32, jnp.bfloat16


def remote(src, dst, send, recv, **where):
    return pltpu.make_async_remote_copy(
        src_ref=src, dst_ref=dst, send_sem=send, recv_sem=recv, device_id=where, device_id_type=MESH
    )


def unpack(rows):
    return jnp.concatenate([rows[:, :SHARE], rows[:, SHARE:]], axis=0)


def kernel(
    ny, nz, nc,
    len_ref, hidden, w_up, w_down, gain_ref, leaf_ref, parent_ref,
    embed_out, centers_out, sums_out,
    hv, hp, upv, downv, from_left, from_right, far, pb, near_left, near_right, rs_left, rs_right,
    hid, table, tables, pick_leaf, pick_parent, blocks, lab, wide, zbuf, zrecv, sbuf, srecv, qrecv,
    pbuf, precv,
    local_sem, ag_send, ag_recv, fwd_send, fwd_recv, d2_send, d2_recv, rs_send, rs_recv,
    t_send, t_recv, s1_send, s1_recv, e_send, e_recv, z1_send, z1_recv,
    s2_send, s2_recv, q_send, q_recv, z2_send, z2_recv,
):
    y, z, c, x = (lax.axis_index(a) for a in (AY, AZ, AC, AX))
    plane = ny * nc
    here = y * nc + c
    right, left, across = lax.rem(x + 1, NX), lax.rem(x + NX - 1, NX), lax.rem(x + 2, NX)

    def mate(k):
        other = lax.rem(here + k, plane)
        return lax.div(other, nc), lax.rem(other, nc)

    fetch = pltpu.make_async_copy(hidden, hv, local_sem.at[0])
    fetch.start()
    loads = []
    for i in range(NX):
        rows = pl.ds(pl.multiple_of(lax.rem(x + i, NX) * SHARE, SHARE), SHARE)
        loads.append(pltpu.make_async_copy(w_up.at[rows], upv.at[i], local_sem.at[1 + i]))
    loads.append(pltpu.make_async_copy(w_down, downv, local_sem.at[1 + NX]))
    for load in loads:
        load.start()

    barrier = pltpu.get_barrier_semaphore()
    for k in range(1, NX):
        pl.semaphore_signal(barrier, 1, device_id={AX: lax.rem(x + k, NX)}, device_id_type=MESH)
    for k in range(1, nz):
        pl.semaphore_signal(barrier, 1, device_id={AZ: lax.rem(z + k, nz)}, device_id_type=MESH)

    @pl.loop(1, plane)
    def _(k):
        yy, cc = mate(k)

        @pl.loop(0, NX)
        def _(i):
            pl.semaphore_signal(barrier, 1, device_id={AY: yy, AC: cc, AX: i}, device_id_type=MESH)

    table[...] = jnp.zeros_like(table)
    table[0:1, 0:LAB] = leaf_ref[...]
    table[1:2, 0:LEAF] = parent_ref[...]
    fetch.wait()
    for p in range(PIECES):
        for j in range(NX):
            first = 128 * j + 32 * p
            hp[p, 16 * j : 16 * j + 16, :] = jnp.concatenate(
                [hv[first : first + 16, :], hv[first + 16 : first + 32, :]], axis=1
            )
    pl.semaphore_wait(barrier, NX - 1 + nz - 1 + (plane - 1) * NX)

    to_right, to_left = {AX: right}, {AX: left}
    ag = []
    for p in range(PIECES):
        ag.append((
            remote(hp.at[p], from_left.at[p], ag_send.at[0, p], ag_recv.at[0, p], **to_right),
            remote(hp.at[p], from_right.at[p], ag_send.at[1, p], ag_recv.at[1, p], **to_left),
        ))
        for copy in ag[p]:
            copy.start()
    low, high = pl.ds(0, 32), pl.ds(32, 32)
    fwd = [
        (
            remote(from_right.at[p, low], far.at[p, low], fwd_send.at[0, p], fwd_recv.at[0, p], **to_left),
            remote(from_left.at[p, high], far.at[p, high], fwd_send.at[1, p], fwd_recv.at[1, p], **to_right),
        )
        for p in range(PIECES)
    ]

    def forward(p):
        ag[p][1].wait_recv()
        fwd[p][0].start()
        ag[p][0].wait_recv()
        fwd[p][1].start()

    @pl.loop(1, plane)
    def _(k):
        yy, cc = mate(k)
        remote(table, tables.at[here], t_send, t_recv, **{AY: yy, AC: cc}).start()

    tables[here] = table[...]

    d2 = [
        (
            remote(pb.at[p, across, 0], near_left.at[p], d2_send.at[0, p], d2_recv.at[0, p], **to_right),
            remote(pb.at[p, across, 1], near_right.at[p], d2_send.at[1, p], d2_recv.at[1, p], **to_left),
        )
        for p in range(PIECES)
    ]
    rs = [
        (
            remote(pb.at[p, right], rs_left.at[p], rs_send.at[0, p], rs_recv.at[0, p], **to_right),
            remote(pb.at[p, left], rs_right.at[p], rs_send.at[1, p], rs_recv.at[1, p], **to_left),
        )
        for p in range(PIECES)
    ]

    def compute(p):
        refs = (hp.at[p], from_right.at[p], far.at[p], from_left.at[p])
        upward = None
        mine = pl.ds(pl.multiple_of(16 * x, 16), 16)
        for i, ref in enumerate(refs):
            term = jnp.dot(unpack(ref[...]), upv[i], preferred_element_type=F32)
            upward = term if upward is None else upward + term
            hid[lax.rem(x + i, NX), 32 * p : 32 * p + 32, :] = unpack(ref[mine, :])
        activ = (0.5 * upward * (1.0 + lax.erf(upward * (0.5**0.5)))).astype(BF16)
        partial = jnp.dot(activ, downv[...], preferred_element_type=F32).astype(BF16)
        for half in range(2):
            for j in range(NX):
                row = 64 * half + 16 * j
                pb[p, j, half] = partial[row : row + 16]

    def finish(p):
        d2[p][0].wait_recv()
        pb[p, right, 0] = (pb[p, right, 0].astype(F32) + near_left[p].astype(F32)).astype(BF16)
        d2[p][1].wait_recv()
        pb[p, left, 1] = (pb[p, left, 1].astype(F32) + near_right[p].astype(F32)).astype(BF16)
        for copy in rs[p]:
            copy.start()

    forward(0)
    for load in loads:
        load.wait()
    for p in range(PIECES):
        if p + 1 < PIECES:
            forward(p + 1)
        for copy in fwd[p]:
            copy.wait_recv()
        compute(p)
        for copy in d2[p]:
            copy.start()
        if p >= 1:
            finish(p - 1)
    finish(PIECES - 1)

    others = tables.at[pl.ds(0, plane - 1)]
    remote(others, others, t_send, t_recv, **to_right).wait_recv()
    column = nz * LEAF
    row = lax.broadcasted_iota(jnp.int32, (column, 1), 0)
    leaf_of_row = ((y * nz + lax.div(row, LEAF)) * nc + c) * LEAF + lax.rem(row, LEAF)
    row2 = lax.broadcasted_iota(jnp.int32, (nz * PAR, 1), 0)
    parent_of_row = ((y * nz + lax.div(row2, PAR)) * nc + c) * PAR + lax.rem(row2, PAR)
    for k in range(plane):
        pick_leaf[:, LAB * k : LAB * (k + 1)] = (leaf_of_row == tables[k, 0:1, 0:LAB]).astype(F32)
        pick_parent[:, LEAF * k : LEAF * (k + 1)] = (parent_of_row == tables[k, 1:2, 0:LEAF]).astype(F32)

    gain = gain_ref[...]
    position = lax.broadcasted_iota(jnp.int32, (SEQ, 1), 0)
    embeds = []
    for p in range(PIECES):
        for copy in rs[p]:
            copy.wait_recv()
        for half in range(2):
            rows = slice(32 * p + 16 * half, 32 * p + 16 * half + 16)
            residual = jnp.concatenate([hid[s, rows, :].astype(F32) for s in range(NX)], axis=1)
            summed = pb[p, x, half].astype(F32) + rs_left[p, half].astype(F32) + rs_right[p, half].astype(F32)
            mixed = (residual + summed).astype(BF16).astype(F32)
            mean = jnp.mean(mixed, axis=1, keepdims=True)
            centred = mixed - mean
            variance = jnp.mean(centred * centred, axis=1, keepdims=True)
            normed = centred * lax.rsqrt(variance + 1e-05) * gain
            length = len_ref[8 * x + 2 * p + half]
            kept = jnp.where(position < length, normed, 0.0)
            pooled = jnp.sum(kept, axis=0, keepdims=True) / length.astype(F32)
            embeds.append(pooled * lax.rsqrt(jnp.mean(pooled * pooled, axis=1, keepdims=True) + 1e-05))
    embed = jnp.concatenate(embeds, axis=0)
    zero = jnp.zeros((8, PAD - SHARE), F32)
    for s in range(NX):
        part = embed[:, SHARE * s : SHARE * (s + 1)]
        blocks[s] = jnp.concatenate([part, zero], axis=1).astype(BF16)

    @pl.loop(0, plane)
    def _(k):
        yy, cc = mate(k)

        @pl.loop(jnp.where(k == 0, 1, 0), NX)
        def _(i):
            to = lax.rem(x + i, NX)
            remote(blocks.at[to], lab.at[here * NX + x], s1_send, s1_recv, **{AY: yy, AC: cc, AX: to}).start()

    for k in range(1, NX):
        remote(blocks, wide.at[x], e_send.at[k], e_recv.at[NX - k], **{AX: lax.rem(x + k, NX)}).start()
    lab[here * NX + x] = blocks[x]
    wide[x] = blocks[...]

    got = lab.at[pl.ds(0, plane * NX - 1)]
    remote(got, got, s1_send, s1_recv, **to_right).wait_recv()
    labels = lab[...].astype(F32).reshape(plane * LAB, PAD).astype(BF16)
    leaf_part = jnp.dot(pick_leaf[...].astype(BF16), labels, preferred_element_type=F32)
    zbuf[...] = leaf_part.reshape(nz, LEAF, PAD).astype(BF16)
    order = sorted(range(1, nz), key=lambda k: -min(k, nz - k))
    for k in order:
        to = lax.rem(z + k, nz)
        remote(zbuf.at[to], zrecv.at[z], z1_send, z1_recv, **{AZ: to}).start()
    zrecv[z] = zbuf[z]

    for k in range(1, NX):
        remote(blocks, wide.at[x], e_send.at[k], e_recv.at[k], **to_right).wait_recv()
    embed_out[...] = jnp.concatenate(
        [
            jnp.concatenate([wide[s, b].astype(F32)[:, :SHARE] for b in range(NX)], axis=1)
            for s in range(NX)
        ],
        axis=0,
    ).astype(BF16)

    got = zrecv.at[pl.ds(0, nz - 1)]
    remote(got, got, z1_send, z1_recv, **to_right).wait_recv()
    leaf_sum = jnp.sum(zrecv[...].astype(F32), axis=0)
    square = jnp.sum(leaf_sum * leaf_sum, axis=1, keepdims=True)
    lane = lax.broadcasted_iota(jnp.int32, (LEAF, PAD), 1)
    sbuf[...] = jnp.where(lane < SHARE, leaf_sum, square)

    @pl.loop(0, plane)
    def _(k):
        yy, cc = mate(k)

        @pl.loop(1, NX)
        def _(i):
            to = {AY: yy, AC: cc, AX: lax.rem(x + i, NX)}
            remote(sbuf.at[:, pl.ds(128, 128)], qrecv.at[x, here], q_send, q_recv, **to).start()

        @pl.when(k > 0)
        def _():
            remote(sbuf, srecv.at[here], s2_send, s2_recv, **{AY: yy, AC: cc}).start()

    srecv[here] = sbuf[...]
    qrecv[x] = jnp.zeros_like(qrecv[x])
    got = srecv.at[pl.ds(0, plane - 1)]
    remote(got, got, s2_send, s2_recv, **to_right).wait_recv()
    got = qrecv.at[pl.ds(0, NX - 1)]
    remote(got, got, q_send, q_recv, **to_right).wait_recv()
    sums = srecv[...]
    total = sums[:, :, PAD - 1 :] + jnp.sum(qrecv[...], axis=0)[:, :, 127:]
    centers = sums * lax.rsqrt(total / WIDE + 1e-05)
    sbuf_mine = srecv[here]
    total_mine = sbuf_mine[:, PAD - 1 :]
    for s in range(NX):
        total_mine = total_mine + qrecv[s, here][:, 127:]
    centers_out[...] = (sbuf_mine * lax.rsqrt(total_mine / WIDE + 1e-05))[:, :SHARE]
    parent_part = jnp.dot(
        pick_parent[...],
        centers.reshape(plane * LEAF, PAD),
        preferred_element_type=F32,
        precision=lax.Precision.HIGHEST,
    )
    for k in range(nz):
        pbuf[k] = parent_part[PAR * k : PAR * (k + 1)]
    for k in order:
        to = lax.rem(z + k, nz)
        remote(pbuf.at[to], precv.at[z], z2_send, z2_recv, **{AZ: to}).start()
    precv[z] = pbuf[z]
    got = precv.at[pl.ds(0, nz - 1)]
    remote(got, got, z2_send, z2_recv, **to_right).wait_recv()
    sums_out[...] = jnp.sum(precv[...], axis=0)[:, :SHARE]

    for p in range(PIECES):
        for copy in (*ag[p], *fwd[p], *d2[p], *rs[p]):
            copy.wait_send()
    remote(others, others, t_send, t_recv, **to_right).wait_send()
    got = lab.at[pl.ds(0, plane * NX - 1)]
    remote(got, got, s1_send, s1_recv, **to_right).wait_send()
    for k in range(1, NX):
        remote(blocks, wide.at[x], e_send.at[k], e_recv.at[k], **to_right).wait_send()
    got = zrecv.at[pl.ds(0, nz - 1)]
    remote(got, got, z1_send, z1_recv, **to_right).wait_send()
    got = srecv.at[pl.ds(0, plane - 1)]
    remote(got, got, s2_send, s2_recv, **to_right).wait_send()
    got = qrecv.at[pl.ds(0, NX - 1)]
    remote(got, got, q_send, q_recv, **to_right).wait_send()
    got = precv.at[pl.ds(0, nz - 1)]
    remote(got, got, z2_send, z2_recv, **to_right).wait_send()


def local(hidden_in, w_up, w_down, norm_gain, title_length, label_leaf, leaf_parent):
    ny, nz, nc = (lax.axis_size(a) for a in LABELS)
    plane = ny * nc
    vmem, dma = pltpu.VMEM, pltpu.SemaphoreType.DMA
    in_vmem = pl.BlockSpec(memory_space=pltpu.VMEM)
    anywhere = pl.BlockSpec(memory_space=pl.ANY)
    gather = vmem((PIECES, 64, 2 * SHARE), BF16)
    near = vmem((PIECES, 16, WIDE), BF16)
    scattered = vmem((PIECES, 2, 16, WIDE), BF16)
    pair = dma((2, PIECES))
    return pl.pallas_call(
        functools.partial(kernel, ny, nz, nc),
        out_shape=(
            jax.ShapeDtypeStruct((LAB, WIDE), BF16),
            jax.ShapeDtypeStruct((LEAF, SHARE), F32),
            jax.ShapeDtypeStruct((PAR, SHARE), F32),
        ),
        in_specs=[
            pl.BlockSpec(memory_space=pltpu.SMEM),
            anywhere, anywhere, anywhere, in_vmem, in_vmem, in_vmem,
        ],
        out_specs=(in_vmem,) * 3,
        scratch_shapes=[
            vmem((NX * 128, SHARE), BF16),
            gather,
            vmem((NX, SHARE, WIDE), BF16),
            vmem((WIDE, WIDE), BF16),
            gather, gather, gather,
            vmem((PIECES, NX, 2, 16, WIDE), BF16),
            near, near, scattered, scattered,
            vmem((NX, 128, SHARE), BF16),
            vmem((8, 128), jnp.int32),
            vmem((plane, 8, 128), jnp.int32),
            vmem((nz * LEAF, plane * LAB), F32),
            vmem((nz * PAR, plane * LEAF), F32),
            vmem((NX, 8, PAD), BF16),
            vmem((plane * NX, 8, PAD), BF16),
            vmem((NX, NX, 8, PAD), BF16),
            vmem((nz, LEAF, PAD), BF16),
            vmem((nz, LEAF, PAD), BF16),
            vmem((LEAF, PAD), F32),
            vmem((plane, LEAF, PAD), F32),
            vmem((NX, plane, LEAF, 128), F32),
            vmem((nz, PAR, PAD), F32),
            vmem((nz, PAR, PAD), F32),
            dma((2 + NX,)),
            pair, pair, pair, pair, pair, pair, pair, pair,
            dma(()), dma(()), dma(()), dma(()),
            dma((NX,)), dma((NX,)),
            dma(()), dma(()), dma(()), dma(()), dma(()), dma(()), dma(()), dma(()),
        ],
        compiler_params=pltpu.CompilerParams(collective_id=0, has_side_effects=True),
    )(
        title_length,
        hidden_in,
        w_up,
        w_down,
        norm_gain[None, :],
        label_leaf[None, :],
        leaf_parent[None, :],
    )


def solution(mesh):
    labels = mesh.shape["labels"]
    side = 4 if labels == 128 else 2
    split = Mesh(
        mesh.devices.reshape(side, labels // side // 2, 2, mesh.shape["heads"]), (AY, AZ, AC, AX)
    )
    placed = (P(LABELS, AX), P(None, AX), P(AX, None), P(), P(LABELS), P(LABELS), P(LABELS))
    return jax.shard_map(
        local,
        mesh=split,
        in_specs=placed,
        out_specs=(P(LABELS, None), P(LABELS, AX), P(LABELS, AX)),
        check_vma=False,
    )
```

time: 154 us -> 76.4 us (0.50)
  Pallas kernels: 0 us -> 68.4 us
  starting transfers between devices: 47.2 us -> 0 us
  blocking collectives: 44.4 us -> 0 us
  waiting for transfers between devices: 36.4 us -> 0 us
  matrix products: 6.93 us -> 0 us
  other arithmetic: 6.37 us -> 0 us
  local copies, waits for them, and re-layouts: 10.4 us -> 7 us
    pallas_call x0 -> x1, Pallas kernels: none -> 68.4 us  [local(): pl.pallas_call(functools.partial(kernel, ny, nz, nc), out_shape=(jax.Shap...]
    all_to_all x4 -> x0, starting transfers between devices: 47.2 us -> none  [the longest x1 29 us: local(): lax.all_to_all(slot_leaf, LABELS, split_axis=0, concat_axis=0, tiled=True)]
    all_to_all x4 -> x0, blocking collectives: 44.4 us -> none  [the longest x2 19.4 us: copy_for_each(): return lax.all_to_all(copies, axis, split_axis=0, concat_axis=0, tiled=True)]
    all_to_all x4 -> x0, waiting for transfers between devices: 36.4 us -> none  [the longest x1 15.8 us: local(): lax.all_to_all(outgoing, LABELS, split_axis=0, concat_axis=0, tiled=True)]
    dot_general x4 -> x0, matrix products: 6.93 us -> none  [the longest x1 6.13 us: local(): jnp.dot(activ, w_down, preferred_element_type=jnp.float32)]
    convert_element_type x4 -> x0, local copies, waits for them, and re-layouts: 5.75 us -> none  [the longest x2 4.5 us: local(): as_float = mixed.astype(jnp.float32)]
    unnamed x16 -> x4, local copies, waits for them, and re-layouts: 0.05 us -> 5.73 us
    reduce_sum x10 -> x0, other arithmetic: 3.84 us -> none  [the longest x1 1.96 us: pool_rows(): jnp.sum(grouped * keep_mask[:, :, None], axis=1)]
  transfers between devices with their start and end apart: 4 -> 0, of which waited for: 4 -> 0; matrix products, arithmetic and copies ran while one was open for 8% -> 0% of each run, Pallas kernels for 0% -> 0%
where the time goes in v1:
time: 76.4 us; the launch traced here: 76 us
  Pallas kernels  68.4 us (90%)
  local copies, waits for them, and re-layouts  7 us (9%)
    pallas_call x1, Pallas kernels, local(): pl.pallas_call(functools.partial(kernel, ny, nz, nc), out_shape=(jax.Shap...  68.4 us
    unnamed x4, local copies, waits for them, and re-layouts  5.73 us

profile of v1, /device:TPU:1, one launch (start us, length us, event | category | flops | bytes accessed | tf_op | source)
XLA Modules:
  0.0 76.0 jit_solution(2901331156697005625)
XLA Ops:
  0.6 1.3 %broadcast_in_dim.9.gain_ref = f32[1,768]{1,0:T(1,128)} reshape(f32[768]{0:T(1024)} %param.10) | data formatting | bytes 6144 | tf_op jit(solution)/shard_map/broadcast_in_dim | solution.py:372
  1.9 1.8 %copy.10.hidden = bf16[512,192]{1,0:T(8,128)(2,1)} copy(bf16[512,192]{0,1:T(8,128)(2,1)} %param.7) | data formatting | bytes 393216 | tf_op args[0]
  3.7 68.4 %shard_map.94 = (bf16[32,768]{1,0:T(8,128)(2,1)}, f32[8,192]{1,0:T(8,128)}, f32[2,192]{1,0:T(2,128)}) custom-call(s32[32]{0:T(128)} %len_ref.1, bf16[512,192]{1,0:T(8,128)(2,1)} %copy.10.hidden, bf16[768,768]{1,0:T(8,128)(2,1)} %w_up.1, bf16[768,768]{1,0:T(8,128)(2,1)} %w_down.1, f32[1,768]{1,0:T(1,128)} %broadcast_in_dim.9.gain_ref, s32[1,32]{1,0:T(1,128)} %bitcast.2, ...), custom_call_target="tpu_custom_call" | custom-call | tf_op jit(solution)/shard_map/pallas_call | solution.py:325
  72.1 1.4 %copy.14 = bf16[32,768]{1,0:T(8,128)(2,1)} copy(bf16[32,768]{1,0:T(8,128)(2,1)} %get-tuple-element.6) | data formatting | bytes 98304
  73.5 1.3 %copy.15 = f32[8,192]{1,0:T(8,128)} copy(f32[8,192]{1,0:T(8,128)} %get-tuple-element.7) | data formatting | bytes 12288
  74.8 1.3 %copy.16 = f32[2,192]{1,0:T(2,128)} copy(f32[2,192]{1,0:T(2,128)} %get-tuple-element.8) | data formatting | bytes 3072

commit v2 on v1

v2 whole, which is shorter than its diff:
```python
import functools

import jax
import jax.numpy as jnp
from jax import lax
from jax.experimental import pallas as pl
from jax.experimental.pallas import tpu as pltpu
from jax.sharding import Mesh
from jax.sharding import PartitionSpec as P

AY, AZ, AC, AX = "labels_0", "labels_1", "labels_2", "heads"
LABELS = (AY, AZ, AC)
NX = 4
SEQ = 16
LAB = 32
LEAF = 8
PAR = 2
PIECES = 4
TOK = 128
OWN = TOK // NX
SHARE = 192
WIDE = 768
PAD = 256
MESH = pl.DeviceIdType.MESH
F32, BF16 = jnp.float32, jnp.bfloat16


def remote(src, dst, send, recv, **where):
    return pltpu.make_async_remote_copy(
        src_ref=src, dst_ref=dst, send_sem=send, recv_sem=recv, device_id=where, device_id_type=MESH
    )


def kernel(
    ny, nz, nc,
    len_ref, hidden, w_up, w_down, gain_ref, leaf_ref, parent_ref,
    embed_out, centers_out, sums_out,
    xg, xt, upv, downv, pb, rsr, table, tables, pick_leaf, pick_parent, blocks, lab, wide,
    zbuf, zrecv, sbuf, srecv, qrecv, pbuf, precv,
    near_y, far_y, other_c, hops_z,
    local_sem, ag_send, ag_recv, rs_send, rs_recv,
    t_send, t_recv, s1_send, s1_recv, e_send, e_recv, z1_send, z1_recv,
    s2_send, s2_recv, q_send, q_recv, z2_send, z2_recv,
):
    y, z, c, x = (lax.axis_index(a) for a in (AY, AZ, AC, AX))
    plane = ny * nc
    here = y * nc + c
    right = {AX: lax.rem(x + 1, NX)}
    mates = [
        (lax.rem(y + dy, ny), lax.rem(c + dc, nc))
        for dy in sorted(range(ny), key=lambda d: -min(d, ny - d))
        for dc in reversed(range(nc))
    ]
    z_order = sorted(range(1, nz), key=lambda k: -min(k, nz - k))
    x_order = (2, 1, 3, 0)
    drain = []

    def signal(sem, **where):
        pl.semaphore_signal(sem, 1, device_id=where, device_id_type=MESH)

    def around(axis, at, size, step, sem):
        signal(sem, **{axis: lax.rem(at + step, size)})
        signal(sem, **{axis: lax.rem(at + size - step, size)})

    barrier = pltpu.get_barrier_semaphore()
    for k in (2, 1, 3):
        signal(barrier, **{AX: lax.rem(x + k, NX)})
    around(AY, y, ny, 1, barrier)
    around(AZ, z, nz, 1, barrier)
    signal(barrier, **{AC: 1 - c})
    loads = []
    for p in range(PIECES):
        cols = hidden.at[:, pl.ds(TOK * p, TOK)]
        loads.append(pltpu.make_async_copy(cols, xg.at[p, x], local_sem.at[p]))
    loads.append(pltpu.make_async_copy(w_up, upv, local_sem.at[PIECES]))
    loads.append(pltpu.make_async_copy(w_down, downv, local_sem.at[PIECES + 1]))
    for load in loads:
        load.start()
    pl.semaphore_wait(barrier, 8)

    ag = []
    for p in range(PIECES):
        for k in (2, 1, 3):
            cols = hidden.at[:, pl.ds(TOK * p, TOK)]
            to = {AX: lax.rem(x + k, NX)}
            ag.append(remote(cols, xg.at[p, x], ag_send.at[p, k], ag_recv.at[p, k], **to))
            ag[-1].start()
            drain.append(ag[-1].wait_send)

    around(AY, y, ny, 1, near_y)
    steps = [s for s in (1, 2, 4) if 2 * s <= nz // 2]
    if steps:
        around(AZ, z, nz, steps[0], hops_z.at[0])

    def handshake_2():
        pl.semaphore_wait(near_y, 2)
        around(AY, y, ny, 1, far_y)
        if len(steps) > 0:
            pl.semaphore_wait(hops_z.at[0], 2)
        if len(steps) > 1:
            around(AZ, z, nz, steps[1], hops_z.at[1])

    def handshake_3():
        pl.semaphore_wait(far_y, 2)
        signal(other_c, **{AC: 1 - c})
        if len(steps) > 1:
            pl.semaphore_wait(hops_z.at[1], 2)
        if len(steps) > 2:
            around(AZ, z, nz, steps[2], hops_z.at[2])

    def handshake_4():
        pl.semaphore_wait(other_c, 1)
        if len(steps) > 2:
            pl.semaphore_wait(hops_z.at[2], 2)

    row = lax.broadcasted_iota(jnp.int32, (LAB, LAB), 0)
    col = lax.broadcasted_iota(jnp.int32, (LAB, LAB), 1)
    inner = lax.rem(col, 8)
    natural = 8 * lax.div(inner, 2) + 2 * lax.div(col, 8) + lax.rem(inner, 2)
    leaves = jnp.broadcast_to(leaf_ref[...], (8, LAB)).astype(F32)
    ordered = jnp.dot(
        leaves, (row == natural).astype(F32), preferred_element_type=F32, precision=lax.Precision.HIGHEST
    )
    table[...] = jnp.zeros_like(table)
    table[0:1, 0:LAB] = ordered[0:1].astype(jnp.int32)
    table[1:2, 0:LEAF] = parent_ref[...]

    rs = {}

    def compute(p):
        features = xg[p].reshape(WIDE, TOK).T
        xt[p] = features
        upward = jnp.dot(features, upv[...], preferred_element_type=F32)
        activ = (0.5 * upward * (1.0 + lax.erf(upward * (0.5**0.5)))).astype(BF16)
        partial = jnp.dot(activ, downv[...], preferred_element_type=F32).astype(BF16)
        for j in range(NX):
            pb[p, j] = partial[OWN * j : OWN * (j + 1)]
        for k in (2, 1, 3):
            to = lax.rem(x + k, NX)
            rs[p, k] = remote(pb.at[p, to], rsr.at[p, k - 1], rs_send.at[p, k], rs_recv.at[p, k], **{AX: to})
            rs[p, k].start()
            drain.append(rs[p, k].wait_send)

    for load in loads:
        load.wait()
    for p in range(PIECES):
        for copy in ag[3 * p : 3 * p + 3]:
            copy.wait_recv()
        compute(p)
        if p == 0:
            handshake_2()
        if p == 2:
            handshake_3()
    handshake_4()

    for yy, cc in mates[:-1]:
        remote(table, tables.at[here], t_send, t_recv, **{AY: yy, AC: cc}).start()
    tables[here] = table[...]

    gain = gain_ref[...].reshape(1, WIDE)
    position = lax.broadcasted_iota(jnp.int32, (SEQ, 1), 0)
    embeds = []

    def pool(p):
        for k in (2, 1, 3):
            rs[p, k].wait_recv()
        for half in range(2):
            rows = pl.ds(pl.multiple_of(OWN * x + SEQ * half, SEQ), SEQ)
            there = pl.ds(SEQ * half, SEQ)
            summed = pb[p, x, there].astype(F32)
            for k in range(NX - 1):
                summed = summed + rsr[p, k, there].astype(F32)
            mixed = (xt[p, rows].astype(F32) + summed).astype(BF16).astype(F32)
            mean = jnp.mean(mixed, axis=1, keepdims=True)
            centred = mixed - mean
            variance = jnp.mean(centred * centred, axis=1, keepdims=True)
            normed = centred * lax.rsqrt(variance + 1e-05) * gain
            length = len_ref[8 * p + 2 * x + half]
            kept = jnp.where(position < length, normed, 0.0)
            pooled = jnp.sum(kept, axis=0, keepdims=True) / length.astype(F32)
            embeds.append(pooled * lax.rsqrt(jnp.mean(pooled * pooled, axis=1, keepdims=True) + 1e-05))

    for p in range(PIECES):
        pool(p)
    embed = jnp.concatenate(embeds, axis=0)
    zero = jnp.zeros((8, PAD - SHARE), F32)
    for s in range(NX):
        part = embed[:, SHARE * s : SHARE * (s + 1)]
        blocks[s] = jnp.concatenate([part, zero], axis=1).astype(BF16)

    slot = here * NX + x
    for n, (yy, cc) in enumerate(mates):
        for k in x_order:
            if k == 0 and n == plane - 1:
                continue
            to = lax.rem(x + k, NX)
            remote(blocks.at[to], lab.at[slot], s1_send, s1_recv, **{AY: yy, AC: cc, AX: to}).start()
    spread = []
    for k in (2, 1, 3):
        to = {AX: lax.rem(x + k, NX)}
        spread.append(remote(blocks, wide.at[x], e_send.at[k], e_recv.at[k], **to))
        spread[-1].start()
        drain.append(spread[-1].wait_send)
    lab[slot] = blocks[x]
    wide[x] = blocks[...]

    others = tables.at[pl.ds(0, plane - 1)]
    others = remote(others, others, t_send, t_recv, **right)
    others.wait_recv()
    drain.append(others.wait_send)
    column = nz * LEAF
    row = lax.broadcasted_iota(jnp.int32, (column, 1), 0)
    leaf_of_row = ((y * nz + lax.div(row, LEAF)) * nc + c) * LEAF + lax.rem(row, LEAF)
    row2 = lax.broadcasted_iota(jnp.int32, (nz * PAR, 1), 0)
    parent_of_row = ((y * nz + lax.div(row2, PAR)) * nc + c) * PAR + lax.rem(row2, PAR)
    for k in range(plane):
        pick_leaf[:, LAB * k : LAB * (k + 1)] = (leaf_of_row == tables[k, 0:1, 0:LAB]).astype(F32)
        pick = (parent_of_row == tables[k, 1:2, 0:LEAF]).astype(F32)
        for part in range(3):
            first = (plane * part + k) * LEAF
            pick_parent[:, first : first + LEAF] = pick
    picked_leaf = pick_leaf[...].astype(BF16)

    got = lab.at[pl.ds(0, plane * NX - 1)]
    got = remote(got, got, s1_send, s1_recv, **right)
    drain.append(got.wait_send)
    got.wait_recv()
    labels = lab[...].astype(F32).reshape(plane * LAB, PAD).astype(BF16)
    leaf_part = jnp.dot(picked_leaf, labels, preferred_element_type=F32)
    zbuf[...] = leaf_part.reshape(nz, LEAF, PAD).astype(BF16)
    for k in z_order:
        to = lax.rem(z + k, nz)
        remote(zbuf.at[to], zrecv.at[z], z1_send, z1_recv, **{AZ: to}).start()
    zrecv[z] = zbuf[z]

    for copy in spread:
        copy.wait_recv()
    whole = [
        jnp.concatenate([wide[s, b].astype(F32)[:, :SHARE] for b in range(NX)], axis=1) for s in range(NX)
    ]
    embed_out[...] = jnp.concatenate(
        [whole[s][2 * p : 2 * p + 2] for p in range(PIECES) for s in range(NX)], axis=0
    ).astype(BF16)

    got = zrecv.at[pl.ds(0, nz - 1)]
    got = remote(got, got, z1_send, z1_recv, **right)
    drain.append(got.wait_send)
    got.wait_recv()
    leaf_sum = jnp.sum(zrecv[...].astype(F32), axis=0)
    square = jnp.sum(leaf_sum * leaf_sum, axis=1, keepdims=True)
    lane = lax.broadcasted_iota(jnp.int32, (LEAF, PAD), 1)
    sbuf[...] = jnp.where(lane < SHARE, leaf_sum, square)

    for n, (yy, cc) in enumerate(mates):
        for k in x_order:
            to = {AY: yy, AC: cc, AX: lax.rem(x + k, NX)}
            if k > 0:
                remote(sbuf.at[:, pl.ds(128, 128)], qrecv.at[x, here], q_send, q_recv, **to).start()
            elif n < plane - 1:
                remote(sbuf, srecv.at[here], s2_send, s2_recv, **to).start()
    srecv[here] = sbuf[...]
    qrecv[x] = jnp.zeros_like(qrecv[x])
    got = srecv.at[pl.ds(0, plane - 1)]
    got = remote(got, got, s2_send, s2_recv, **right)
    drain.append(got.wait_send)
    got.wait_recv()
    got = qrecv.at[pl.ds(0, NX - 1)]
    got = remote(got, got, q_send, q_recv, **right)
    drain.append(got.wait_send)
    got.wait_recv()
    sums = srecv[...]
    total = sums[:, :, PAD - 1 :] + jnp.sum(qrecv[...], axis=0)[:, :, 127:]
    centers = (sums * lax.rsqrt(total / WIDE + 1e-05)).reshape(plane * LEAF, PAD)
    parts = []
    rest = centers
    for part in range(3):
        parts.append(rest.astype(BF16))
        rest = rest - parts[-1].astype(F32)
    parent_part = jnp.dot(
        pick_parent[...].astype(BF16), jnp.concatenate(parts, axis=0), preferred_element_type=F32
    )
    for k in range(nz):
        pbuf[k] = parent_part[PAR * k : PAR * (k + 1)]
    for k in z_order:
        to = lax.rem(z + k, nz)
        remote(pbuf.at[to], precv.at[z], z2_send, z2_recv, **{AZ: to}).start()
    precv[z] = pbuf[z]
    mine = srecv[here]
    total = mine[:, PAD - 1 :]
    for s in range(NX):
        total = total + qrecv[s, here][:, 127:]
    centers_out[...] = (mine * lax.rsqrt(total / WIDE + 1e-05))[:, :SHARE]
    got = precv.at[pl.ds(0, nz - 1)]
    got = remote(got, got, z2_send, z2_recv, **right)
    drain.append(got.wait_send)
    got.wait_recv()
    sums_out[...] = jnp.sum(precv[...], axis=0)[:, :SHARE]
    for wait in drain:
        wait()


def hand_over(*refs):
    ins, outs, sem = refs[:3], refs[3:6], refs[6]
    copies = [pltpu.make_async_copy(a, b, sem.at[i]) for i, (a, b) in enumerate(zip(ins, outs))]
    for copy in copies:
        copy.start()
    for copy in copies:
        copy.wait()


def local(hidden_in, w_up, w_down, norm_gain, title_length, label_leaf, leaf_parent):
    ny, nz, nc = (lax.axis_size(a) for a in LABELS)
    plane = ny * nc
    vmem, dma, regular = pltpu.VMEM, pltpu.SemaphoreType.DMA, pltpu.SemaphoreType.REGULAR
    in_vmem = pl.BlockSpec(memory_space=pltpu.VMEM)
    anywhere = pl.BlockSpec(memory_space=pl.ANY)
    out_shape = (
        jax.ShapeDtypeStruct((LAB, WIDE), BF16),
        jax.ShapeDtypeStruct((LEAF, SHARE), F32),
        jax.ShapeDtypeStruct((PAR, SHARE), F32),
    )
    outs = pl.pallas_call(
        functools.partial(kernel, ny, nz, nc),
        out_shape=out_shape,
        in_specs=[
            pl.BlockSpec(memory_space=pltpu.SMEM),
            anywhere, anywhere, anywhere, in_vmem, in_vmem, in_vmem,
        ],
        out_specs=(in_vmem,) * 3,
        scratch_shapes=[
            vmem((PIECES, NX, SHARE, TOK), BF16),
            vmem((PIECES, TOK, WIDE), BF16),
            vmem((WIDE, WIDE), BF16),
            vmem((WIDE, WIDE), BF16),
            vmem((PIECES, NX, OWN, WIDE), BF16),
            vmem((PIECES, NX - 1, OWN, WIDE), BF16),
            vmem((8, 128), jnp.int32),
            vmem((plane, 8, 128), jnp.int32),
            vmem((nz * LEAF, plane * LAB), F32),
            vmem((nz * PAR, 3 * plane * LEAF), F32),
            vmem((NX, 8, PAD), BF16),
            vmem((plane * NX, 8, PAD), BF16),
            vmem((NX, NX, 8, PAD), BF16),
            vmem((nz, LEAF, PAD), BF16),
            vmem((nz, LEAF, PAD), BF16),
            vmem((LEAF, PAD), F32),
            vmem((plane, LEAF, PAD), F32),
            vmem((NX, plane, LEAF, 128), F32),
            vmem((nz, PAR, PAD), F32),
            vmem((nz, PAR, PAD), F32),
            regular, regular, regular, regular((3,)),
            dma((PIECES + 2,)),
            dma((PIECES, NX)), dma((PIECES, NX)), dma((PIECES, NX)), dma((PIECES, NX)),
            dma(()), dma(()), dma(()), dma(()),
            dma((NX,)), dma((NX,)),
            dma(()), dma(()), dma(()), dma(()), dma(()), dma(()), dma(()), dma(()),
        ],
        compiler_params=pltpu.CompilerParams(collective_id=0, has_side_effects=True),
    )(
        title_length,
        hidden_in.T,
        w_up,
        w_down,
        norm_gain,
        label_leaf[None, :],
        leaf_parent[None, :],
    )
    return pl.pallas_call(
        hand_over,
        out_shape=out_shape,
        in_specs=[anywhere] * 3,
        out_specs=(anywhere,) * 3,
        scratch_shapes=[dma((3,))],
    )(*outs)


def solution(mesh):
    labels = mesh.shape["labels"]
    side = 4 if labels == 128 else 2
    split = Mesh(
        mesh.devices.reshape(side, labels // side // 2, 2, mesh.shape["heads"]), (AY, AZ, AC, AX)
    )
    placed = (P(LABELS, AX), P(None, AX), P(AX, None), P(), P(LABELS), P(LABELS), P(LABELS))
    return jax.shard_map(
        local,
        mesh=split,
        in_specs=placed,
        out_specs=(P(LABELS, None), P(LABELS, AX), P(LABELS, AX)),
        check_vma=False,
    )
```

time: 76.4 us -> 62.1 us (0.81)
  Pallas kernels: 68.4 us -> 61.3 us
  local copies, waits for them, and re-layouts: 7 us -> 0 us
    pallas_call x1 -> x2, Pallas kernels: 68.4 us -> 61.3 us  [the longest x1 58.4 us: local(): pl.pallas_call(functools.partial(kernel, ny, nz, nc), out_shape=out_shape...]
    unnamed x4 -> x0, local copies, waits for them, and re-layouts: 5.73 us -> none
    broadcast_in_dim x1 -> x0, local copies, waits for them, and re-layouts: 1.27 us -> none  [local(): norm_gain[None, :]]
where the time goes in v2:
time: 62.1 us; the launch traced here: 61.9 us
  Pallas kernels  61.3 us (99%)
  between operations  0.64 us (1%)
    pallas_call x1, Pallas kernels, local(): pl.pallas_call(functools.partial(kernel, ny, nz, nc), out_shape=out_shape...  58.4 us
    pallas_call x1, Pallas kernels, local(): pl.pallas_call(hand_over, out_shape=out_shape, in_specs=[anywhere] * 3, o...  2.93 us

profile of v2, /device:TPU:1, one launch (start us, length us, event | category | flops | bytes accessed | tf_op | source)
XLA Modules:
  0.0 61.9 jit_solution(7261021153841231439)
XLA Ops:
  0.6 58.4 %shard_map.94 = (bf16[32,768]{1,0:T(8,128)(2,1)}, f32[8,192]{1,0:T(8,128)}, f32[2,192]{1,0:T(2,128)}) custom-call(s32[32]{0:T(128)} %len_ref.1, bf16[192,512]{1,0:T(8,128)(2,1)} %bitcast.3, bf16[768,768]{1,0:T(8,128)(2,1)} %w_up.1, bf16[768,768]{1,0:T(8,128)(2,1)} %w_down.1, f32[768]{0:T(1024)} %gain_ref.1, s32[1,32]{1,0:T(1,128)} %bitcast.4, s32[1,8]{1,0:T(1,128)} %bitcast.5), custom_call_target="tpu_custom_call" | custom-call | tf_op jit(solution)/shard_map/pallas_call | solution.py:322
  59.0 2.9 %shard_map.95 = (bf16[32,768]{1,0:T(8,128)(2,1)}, f32[8,192]{1,0:T(8,128)}, f32[2,192]{1,0:T(2,128)}) custom-call(bf16[32,768]{1,0:T(8,128)(2,1)} %get-tuple-element.6.refs_0_, f32[8,192]{1,0:T(8,128)} %get-tuple-element.7.refs_1_, f32[2,192]{1,0:T(2,128)} %get-tuple-element.8.refs_2_), custom_call_target="tpu_custom_call" | custom-call | tf_op jit(solution)/shard_map/pallas_call | solution.py:368

commit v3 on v2

--- a/solution.py
+++ b/solution.py
@@ -300,12 +300,9 @@
 
 
 def hand_over(*refs):
-    ins, outs, sem = refs[:3], refs[3:6], refs[6]
-    copies = [pltpu.make_async_copy(a, b, sem.at[i]) for i, (a, b) in enumerate(zip(ins, outs))]
-    for copy in copies:
-        copy.start()
-    for copy in copies:
-        copy.wait()
+    ins, outs = refs[:3], refs[3:6]
+    for a, b in zip(ins, outs):
+        b[...] = a[...]
 
 
 def local(hidden_in, w_up, w_down, norm_gain, title_length, label_leaf, leaf_parent):
@@ -321,7 +318,7 @@
     )
     outs = pl.pallas_call(
         functools.partial(kernel, ny, nz, nc),
-        out_shape=out_shape,
+        out_shape=tuple(vmem(o.shape, o.dtype) for o in out_shape),
         in_specs=[
             pl.BlockSpec(memory_space=pltpu.SMEM),
             anywhere, anywhere, anywhere, in_vmem, in_vmem, in_vmem,
@@ -368,10 +365,9 @@
     return pl.pallas_call(
         hand_over,
         out_shape=out_shape,
-        in_specs=[anywhere] * 3,
-        out_specs=(anywhere,) * 3,
-        scratch_shapes=[dma((3,))],
-    )(*outs)
+        in_specs=[in_vmem] * 3,
+        out_specs=(in_vmem,) * 3,
+    )(*(pltpu.with_memory_space_constraint(o, pltpu.VMEM) for o in outs))
 
 
 def solution(mesh):

time: 62.1 us -> 59.2 us (0.953)
  Pallas kernels: 61.3 us -> 58.4 us
    pallas_call x2, Pallas kernels: 61.3 us -> 58.4 us  [the longest x1 57.7 us: local(): pl.pallas_call(functools.partial(kernel, ny, nz, nc), out_shape=tuple((vm...]
where the time goes in v3:
time: 59.2 us; the launch traced here: 59 us
  Pallas kernels  58.4 us (99%)
  between operations  0.64 us (1%)
    pallas_call x1, Pallas kernels, local(): pl.pallas_call(functools.partial(kernel, ny, nz, nc), out_shape=tuple((vm...  57.7 us

profile of v3, /device:TPU:1, one launch (start us, length us, event | category | flops | bytes accessed | tf_op | source)
XLA Modules:
  0.0 59.0 jit_solution(12591132716538822445)
XLA Ops:
  0.6 57.7 %shard_map.94 = (bf16[32,768]{1,0:T(8,128)(2,1)S(1)}, f32[8,192]{1,0:T(8,128)S(1)}, f32[2,192]{1,0:T(2,128)S(1)}) custom-call(s32[32]{0:T(128)} %len_ref.1, bf16[192,512]{1,0:T(8,128)(2,1)} %bitcast.3, bf16[768,768]{1,0:T(8,128)(2,1)} %w_up.1, bf16[768,768]{1,0:T(8,128)(2,1)} %w_down.1, f32[768]{0:T(1024)} %gain_ref.1, s32[1,32]{1,0:T(1,128)} %bitcast.4, ...), custom_call_target="tpu_custom_call" | custom-call | tf_op jit(solution)/shard_map/pallas_call | solution.py:319
  58.4 0.6 %shard_map.95 = (bf16[32,768]{1,0:T(8,128)(2,1)}, f32[8,192]{1,0:T(8,128)}, f32[2,192]{1,0:T(2,128)}) custom-call(bf16[32,768]{1,0:T(8,128)(2,1)S(1)} %get-tuple-element.6.refs_0_, f32[8,192]{1,0:T(8,128)S(1)} %get-tuple-element.7.refs_1_, f32[2,192]{1,0:T(2,128)S(1)} %get-tuple-element.8.refs_2_), custom_call_target="tpu_custom_call" | custom-call | tf_op jit(solution)/shard_map/pallas_call | solution.py:365

commit v4 on v3

--- a/solution.py
+++ b/solution.py
@@ -15,6 +15,7 @@
 LAB = 32
 LEAF = 8
 PAR = 2
+JOINED = (0, 1, 2)
 PIECES = 4
 TOK = 128
 OWN = TOK // NX
@@ -33,13 +34,13 @@
 
 def kernel(
     ny, nz, nc,
-    len_ref, hidden, w_up, w_down, gain_ref, leaf_ref, parent_ref,
+    length_in, hidden, w_up, w_down, gain_in, leaf_in, parent_in,
     embed_out, centers_out, sums_out,
-    xg, xt, upv, downv, pb, rsr, table, tables, pick_leaf, pick_parent, blocks, lab, wide,
+    len_ref, gain_ref, leaf_ref, parent_ref, xg, xt, upv, downv, pb, rsr, near, table, tables, pick_leaf, pick_parent, blocks, lab, wide,
     zbuf, zrecv, sbuf, srecv, qrecv, pbuf, precv,
     near_y, far_y, other_c, hops_z,
-    local_sem, ag_send, ag_recv, rs_send, rs_recv,
-    t_send, t_recv, s1_send, s1_recv, e_send, e_recv, z1_send, z1_recv,
+    local_sem, ag_send, ag_recv, rs_send, rs_recv, d2_send, d2_recv,
+    n_send, n_recv, t_send, t_recv, s1_send, s1_recv, e_send, e_recv, z1_send, z1_recv,
     s2_send, s2_recv, q_send, q_recv, z2_send, z2_recv,
 ):
     y, z, c, x = (lax.axis_index(a) for a in (AY, AZ, AC, AX))
@@ -74,7 +75,13 @@
         loads.append(pltpu.make_async_copy(cols, xg.at[p, x], local_sem.at[p]))
     loads.append(pltpu.make_async_copy(w_up, upv, local_sem.at[PIECES]))
     loads.append(pltpu.make_async_copy(w_down, downv, local_sem.at[PIECES + 1]))
-    for load in loads:
+    small = [
+        pltpu.make_async_copy(a, b, local_sem.at[PIECES + 2 + i])
+        for i, (a, b) in enumerate(
+            ((leaf_in, leaf_ref), (parent_in, parent_ref), (gain_in, gain_ref), (length_in, len_ref))
+        )
+    ]
+    for load in small + loads:
         load.start()
     pl.semaphore_wait(barrier, 8)
 
@@ -117,6 +124,8 @@
     col = lax.broadcasted_iota(jnp.int32, (LAB, LAB), 1)
     inner = lax.rem(col, 8)
     natural = 8 * lax.div(inner, 2) + 2 * lax.div(col, 8) + lax.rem(inner, 2)
+    for load in small:
+        load.wait()
     leaves = jnp.broadcast_to(leaf_ref[...], (8, LAB)).astype(F32)
     ordered = jnp.dot(
         leaves, (row == natural).astype(F32), preferred_element_type=F32, precision=lax.Precision.HIGHEST
@@ -125,7 +134,8 @@
     table[0:1, 0:LAB] = ordered[0:1].astype(jnp.int32)
     table[1:2, 0:LEAF] = parent_ref[...]
 
-    rs = {}
+    joins, arrivals = {}, {}
+    waits = []
 
     def compute(p):
         features = xg[p].reshape(WIDE, TOK).T
@@ -135,22 +145,56 @@
         partial = jnp.dot(activ, downv[...], preferred_element_type=F32).astype(BF16)
         for j in range(NX):
             pb[p, j] = partial[OWN * j : OWN * (j + 1)]
+        if p in JOINED:
+            join(p)
+            return
         for k in (2, 1, 3):
             to = lax.rem(x + k, NX)
-            rs[p, k] = remote(pb.at[p, to], rsr.at[p, k - 1], rs_send.at[p, k], rs_recv.at[p, k], **{AX: to})
-            rs[p, k].start()
-            drain.append(rs[p, k].wait_send)
+            launch(pb.at[p, to], rsr.at[p, k - 1], rs_send.at[p, k], rs_recv.at[p, k], to)
+
+    low, high = pl.ds(0, SEQ), pl.ds(SEQ, SEQ)
+    across = lax.rem(x + 2, NX)
+    sides = tuple((k, lax.rem(x + k, NX), *rows) for k, rows in ((1, (low, high)), (3, (high, low))))
+
+    def launch(src, dst, send, recv, to):
+        copy = remote(src, dst, send, recv, **{AX: to})
+        copy.start()
+        drain.append(copy.wait_send)
+        waits[0].append(copy.wait_recv)
+
+    def join(p):
+        n = JOINED.index(p)
+        for k, to, through, plain in sides:
+            joins[p, k] = remote(
+                pb.at[p, across, through], near.at[n, through], d2_send.at[n, k], d2_recv.at[n, k], **{AX: to}
+            )
+            joins[p, k].start()
+            drain.append(joins[p, k].wait_send)
+        for k, to, through, plain in sides:
+            launch(pb.at[p, to, plain], rsr.at[p, k - 1, plain], n_send.at[n, k], n_recv.at[n, k], to)
+
+    def finish(p):
+        n = JOINED.index(p)
+        for k, to, through, plain in sides:
+            joins[p, k].wait_recv()
+            both = pb[p, to, through].astype(F32) + near[n, through].astype(F32)
+            pb[p, to, through] = both.astype(BF16)
+            launch(pb.at[p, to, through], rsr.at[p, k - 1, through], rs_send.at[p, k], rs_recv.at[p, k], to)
 
     for load in loads:
         load.wait()
     for p in range(PIECES):
         for copy in ag[3 * p : 3 * p + 3]:
             copy.wait_recv()
+        waits[:] = [arrivals.setdefault(p, [])]
         compute(p)
         if p == 0:
             handshake_2()
         if p == 2:
             handshake_3()
+    for p in JOINED:
+        waits[:] = [arrivals[p]]
+        finish(p)
     handshake_4()
 
     for yy, cc in mates[:-1]:
@@ -159,16 +203,16 @@
 
     gain = gain_ref[...].reshape(1, WIDE)
     position = lax.broadcasted_iota(jnp.int32, (SEQ, 1), 0)
-    embeds = []
+    embeds = {}
 
     def pool(p):
-        for k in (2, 1, 3):
-            rs[p, k].wait_recv()
+        for wait in arrivals[p]:
+            wait()
         for half in range(2):
             rows = pl.ds(pl.multiple_of(OWN * x + SEQ * half, SEQ), SEQ)
             there = pl.ds(SEQ * half, SEQ)
             summed = pb[p, x, there].astype(F32)
-            for k in range(NX - 1):
+            for k in (0, 2) if p in JOINED else range(NX - 1):
                 summed = summed + rsr[p, k, there].astype(F32)
             mixed = (xt[p, rows].astype(F32) + summed).astype(BF16).astype(F32)
             mean = jnp.mean(mixed, axis=1, keepdims=True)
@@ -178,11 +222,12 @@
             length = len_ref[8 * p + 2 * x + half]
             kept = jnp.where(position < length, normed, 0.0)
             pooled = jnp.sum(kept, axis=0, keepdims=True) / length.astype(F32)
-            embeds.append(pooled * lax.rsqrt(jnp.mean(pooled * pooled, axis=1, keepdims=True) + 1e-05))
-
-    for p in range(PIECES):
+            scale = lax.rsqrt(jnp.mean(pooled * pooled, axis=1, keepdims=True) + 1e-05)
+            embeds[p, half] = pooled * scale
+
+    for p in (0, 3, 1, 2):
         pool(p)
-    embed = jnp.concatenate(embeds, axis=0)
+    embed = jnp.concatenate([embeds[p, half] for p in range(PIECES) for half in range(2)], axis=0)
     zero = jnp.zeros((8, PAD - SHARE), F32)
     for s in range(NX):
         part = embed[:, SHARE * s : SHARE * (s + 1)]
@@ -195,12 +240,6 @@
                 continue
             to = lax.rem(x + k, NX)
             remote(blocks.at[to], lab.at[slot], s1_send, s1_recv, **{AY: yy, AC: cc, AX: to}).start()
-    spread = []
-    for k in (2, 1, 3):
-        to = {AX: lax.rem(x + k, NX)}
-        spread.append(remote(blocks, wide.at[x], e_send.at[k], e_recv.at[k], **to))
-        spread[-1].start()
-        drain.append(spread[-1].wait_send)
     lab[slot] = blocks[x]
     wide[x] = blocks[...]
 
@@ -232,6 +271,12 @@
         to = lax.rem(z + k, nz)
         remote(zbuf.at[to], zrecv.at[z], z1_send, z1_recv, **{AZ: to}).start()
     zrecv[z] = zbuf[z]
+    spread = []
+    for k in (2, 1, 3):
+        to = {AX: lax.rem(x + k, NX)}
+        spread.append(remote(blocks, wide.at[x], e_send.at[k], e_recv.at[k], **to))
+        spread[-1].start()
+        drain.append(spread[-1].wait_send)
 
     for copy in spread:
         copy.wait_recv()
@@ -319,18 +364,20 @@
     outs = pl.pallas_call(
         functools.partial(kernel, ny, nz, nc),
         out_shape=tuple(vmem(o.shape, o.dtype) for o in out_shape),
-        in_specs=[
-            pl.BlockSpec(memory_space=pltpu.SMEM),
-            anywhere, anywhere, anywhere, in_vmem, in_vmem, in_vmem,
-        ],
+        in_specs=[anywhere] * 7,
         out_specs=(in_vmem,) * 3,
         scratch_shapes=[
+            pltpu.SMEM((LAB,), jnp.int32),
+            vmem((WIDE,), F32),
+            vmem((1, LAB), jnp.int32),
+            vmem((1, LEAF), jnp.int32),
             vmem((PIECES, NX, SHARE, TOK), BF16),
             vmem((PIECES, TOK, WIDE), BF16),
             vmem((WIDE, WIDE), BF16),
             vmem((WIDE, WIDE), BF16),
             vmem((PIECES, NX, OWN, WIDE), BF16),
             vmem((PIECES, NX - 1, OWN, WIDE), BF16),
+            vmem((len(JOINED), OWN, WIDE), BF16),
             vmem((8, 128), jnp.int32),
             vmem((plane, 8, 128), jnp.int32),
             vmem((nz * LEAF, plane * LAB), F32),
@@ -346,8 +393,9 @@
             vmem((nz, PAR, PAD), F32),
             vmem((nz, PAR, PAD), F32),
             regular, regular, regular, regular((3,)),
-            dma((PIECES + 2,)),
+            dma((PIECES + 6,)),
             dma((PIECES, NX)), dma((PIECES, NX)), dma((PIECES, NX)), dma((PIECES, NX)),
+            dma((3, NX)), dma((3, NX)), dma((3, NX)), dma((3, NX)),
             dma(()), dma(()), dma(()), dma(()),
             dma((NX,)), dma((NX,)),
             dma(()), dma(()), dma(()), dma(()), dma(()), dma(()), dma(()), dma(()),

time: 59.2 us -> 57.5 us (0.971)
  Pallas kernels: 58.4 us -> 56.7 us
    pallas_call x1, Pallas kernels: 57.7 us -> 56.1 us  [local(): pl.pallas_call(functools.partial(kernel, ny, nz, nc), out_shape=tuple((vm...]
where the time goes in v4:
time: 57.5 us; the launch traced here: 57.3 us
  Pallas kernels  56.7 us (99%)
  between operations  0.64 us (1%)
    pallas_call x1, Pallas kernels, local(): pl.pallas_call(functools.partial(kernel, ny, nz, nc), out_shape=tuple((vm...  56.1 us

profile of v4, /device:TPU:1, one launch (start us, length us, event | category | flops | bytes accessed | tf_op | source)
XLA Modules:
  0.0 57.3 jit_solution(10952969508379470101)
XLA Ops:
  0.6 56.1 %shard_map.94 = (bf16[32,768]{1,0:T(8,128)(2,1)S(1)}, f32[8,192]{1,0:T(8,128)S(1)}, f32[2,192]{1,0:T(2,128)S(1)}) custom-call(s32[32]{0:T(128)} %length_in.1, bf16[192,512]{1,0:T(8,128)(2,1)} %bitcast.3, bf16[768,768]{1,0:T(8,128)(2,1)} %w_up.1, bf16[768,768]{1,0:T(8,128)(2,1)} %w_down.1, f32[768]{0:T(1024)} %gain_in.1, s32[1,32]{1,0:T(1,128)} %bitcast.4, ...), custom_call_target="tpu_custom_call" | custom-call | tf_op jit(solution)/shard_map/pallas_call | solution.py:364
  56.7 0.6 %shard_map.95 = (bf16[32,768]{1,0:T(8,128)(2,1)}, f32[8,192]{1,0:T(8,128)}, f32[2,192]{1,0:T(2,128)}) custom-call(bf16[32,768]{1,0:T(8,128)(2,1)S(1)} %get-tuple-element.6.refs_0_, f32[8,192]{1,0:T(8,128)S(1)} %get-tuple-element.7.refs_1_, f32[2,192]{1,0:T(2,128)S(1)} %get-tuple-element.8.refs_2_), custom_call_target="tpu_custom_call" | custom-call | tf_op jit(solution)/shard_map/pallas_call | solution.py:413

commit v5 on v4

--- a/solution.py
+++ b/solution.py
@@ -15,10 +15,10 @@
 LAB = 32
 LEAF = 8
 PAR = 2
-JOINED = (0, 1, 2)
 PIECES = 4
+ROLE = (2, 1, 3, 0)
 TOK = 128
-OWN = TOK // NX
+HALF, PART = TOK // 2, TOK // 4
 SHARE = 192
 WIDE = 768
 PAD = 256
@@ -36,11 +36,11 @@
     ny, nz, nc,
     length_in, hidden, w_up, w_down, gain_in, leaf_in, parent_in,
     embed_out, centers_out, sums_out,
-    len_ref, gain_ref, leaf_ref, parent_ref, xg, xt, upv, downv, pb, rsr, near, table, tables, pick_leaf, pick_parent, blocks, lab, wide,
+    len_ref, gain_ref, leaf_ref, parent_ref, xg, xt, upv, downv, pb, rsl, near, table, tables, pick_leaf, pick_parent, blocks, lab, wide,
     zbuf, zrecv, sbuf, srecv, qrecv, pbuf, precv,
     near_y, far_y, other_c, hops_z,
     local_sem, ag_send, ag_recv, rs_send, rs_recv, d2_send, d2_recv,
-    n_send, n_recv, t_send, t_recv, s1_send, s1_recv, e_send, e_recv, z1_send, z1_recv,
+    t_send, t_recv, s1_send, s1_recv, e_send, e_recv, z1_send, z1_recv,
     s2_send, s2_recv, q_send, q_recv, z2_send, z2_recv,
 ):
     y, z, c, x = (lax.axis_index(a) for a in (AY, AZ, AC, AX))
@@ -70,9 +70,12 @@
     around(AZ, z, nz, 1, barrier)
     signal(barrier, **{AC: 1 - c})
     loads = []
+    def piece_of(device, p):
+        first = pl.multiple_of(lax.rem(device + ROLE[p], NX) * TOK, TOK)
+        return hidden.at[:, pl.ds(first, TOK)]
+
     for p in range(PIECES):
-        cols = hidden.at[:, pl.ds(TOK * p, TOK)]
-        loads.append(pltpu.make_async_copy(cols, xg.at[p, x], local_sem.at[p]))
+        loads.append(pltpu.make_async_copy(piece_of(x, p), xg.at[p, x], local_sem.at[p]))
     loads.append(pltpu.make_async_copy(w_up, upv, local_sem.at[PIECES]))
     loads.append(pltpu.make_async_copy(w_down, downv, local_sem.at[PIECES + 1]))
     small = [
@@ -85,14 +88,18 @@
         load.start()
     pl.semaphore_wait(barrier, 8)
 
-    ag = []
-    for p in range(PIECES):
+    ag = {}
+
+    def gather(p):
         for k in (2, 1, 3):
-            cols = hidden.at[:, pl.ds(TOK * p, TOK)]
-            to = {AX: lax.rem(x + k, NX)}
-            ag.append(remote(cols, xg.at[p, x], ag_send.at[p, k], ag_recv.at[p, k], **to))
-            ag[-1].start()
-            drain.append(ag[-1].wait_send)
+            to = lax.rem(x + k, NX)
+            copy = remote(piece_of(to, p), xg.at[p, x], ag_send.at[p, k], ag_recv.at[p, k], **{AX: to})
+            copy.start()
+            ag[p, k] = copy
+            drain.append(copy.wait_send)
+
+    for p in range(PIECES - 1):
+        gather(p)
 
     around(AY, y, ny, 1, near_y)
     steps = [s for s in (1, 2, 4) if 2 * s <= nz // 2]
@@ -120,81 +127,62 @@
         if len(steps) > 2:
             pl.semaphore_wait(hops_z.at[2], 2)
 
-    row = lax.broadcasted_iota(jnp.int32, (LAB, LAB), 0)
-    col = lax.broadcasted_iota(jnp.int32, (LAB, LAB), 1)
-    inner = lax.rem(col, 8)
-    natural = 8 * lax.div(inner, 2) + 2 * lax.div(col, 8) + lax.rem(inner, 2)
     for load in small:
         load.wait()
-    leaves = jnp.broadcast_to(leaf_ref[...], (8, LAB)).astype(F32)
-    ordered = jnp.dot(
-        leaves, (row == natural).astype(F32), preferred_element_type=F32, precision=lax.Precision.HIGHEST
-    )
     table[...] = jnp.zeros_like(table)
-    table[0:1, 0:LAB] = ordered[0:1].astype(jnp.int32)
+    table[0:1, 0:LAB] = leaf_ref[...]
     table[1:2, 0:LEAF] = parent_ref[...]
 
-    joins, arrivals = {}, {}
-    waits = []
-
     def compute(p):
+        for k in (2, 1, 3):
+            ag[p, k].wait_recv()
         features = xg[p].reshape(WIDE, TOK).T
-        xt[p] = features
+        if p == PIECES - 1:
+            xt[...] = features
         upward = jnp.dot(features, upv[...], preferred_element_type=F32)
         activ = (0.5 * upward * (1.0 + lax.erf(upward * (0.5**0.5)))).astype(BF16)
-        partial = jnp.dot(activ, downv[...], preferred_element_type=F32).astype(BF16)
-        for j in range(NX):
-            pb[p, j] = partial[OWN * j : OWN * (j + 1)]
-        if p in JOINED:
-            join(p)
-            return
-        for k in (2, 1, 3):
-            to = lax.rem(x + k, NX)
-            launch(pb.at[p, to], rsr.at[p, k - 1], rs_send.at[p, k], rs_recv.at[p, k], to)
-
-    low, high = pl.ds(0, SEQ), pl.ds(SEQ, SEQ)
-    across = lax.rem(x + 2, NX)
-    sides = tuple((k, lax.rem(x + k, NX), *rows) for k, rows in ((1, (low, high)), (3, (high, low))))
-
-    def launch(src, dst, send, recv, to):
-        copy = remote(src, dst, send, recv, **{AX: to})
+        pb[p] = jnp.dot(activ, downv[...], preferred_element_type=F32).astype(BF16)
+
+    sides = ((0, 1, 0), (1, 3, HALF))
+    joins, arrivals = {}, []
+
+    def send(src, dst, send_sem, recv_sem, k):
+        copy = remote(src, dst, send_sem, recv_sem, **{AX: lax.rem(x + k, NX)})
         copy.start()
         drain.append(copy.wait_send)
-        waits[0].append(copy.wait_recv)
-
-    def join(p):
-        n = JOINED.index(p)
-        for k, to, through, plain in sides:
-            joins[p, k] = remote(
-                pb.at[p, across, through], near.at[n, through], d2_send.at[n, k], d2_recv.at[n, k], **{AX: to}
+        return copy
+
+    def finish(part):
+        for side, k, first in sides:
+            rows = pl.ds(first + PART * part, PART)
+            joins[side, part].wait_recv()
+            both = pb[1 + side, rows, :].astype(F32) + near[side, part].astype(F32)
+            pb[1 + side, rows, :] = both.astype(BF16)
+            arrivals.append(
+                send(pb.at[1 + side, rows], rsl.at[side, rows], rs_send.at[side, part], rs_recv.at[side, part], k)
             )
-            joins[p, k].start()
-            drain.append(joins[p, k].wait_send)
-        for k, to, through, plain in sides:
-            launch(pb.at[p, to, plain], rsr.at[p, k - 1, plain], n_send.at[n, k], n_recv.at[n, k], to)
-
-    def finish(p):
-        n = JOINED.index(p)
-        for k, to, through, plain in sides:
-            joins[p, k].wait_recv()
-            both = pb[p, to, through].astype(F32) + near[n, through].astype(F32)
-            pb[p, to, through] = both.astype(BF16)
-            launch(pb.at[p, to, through], rsr.at[p, k - 1, through], rs_send.at[p, k], rs_recv.at[p, k], to)
 
     for load in loads:
         load.wait()
-    for p in range(PIECES):
-        for copy in ag[3 * p : 3 * p + 3]:
-            copy.wait_recv()
-        waits[:] = [arrivals.setdefault(p, [])]
-        compute(p)
-        if p == 0:
-            handshake_2()
-        if p == 2:
-            handshake_3()
-    for p in JOINED:
-        waits[:] = [arrivals[p]]
-        finish(p)
+    compute(0)
+    for part in range(2):
+        for side, k, first in sides:
+            rows = pl.ds(first + PART * part, PART)
+            joins[side, part] = send(
+                pb.at[0, rows], near.at[side, part], d2_send.at[side, part], d2_recv.at[side, part], k
+            )
+    gather(PIECES - 1)
+    handshake_2()
+    for side, k, first in sides:
+        compute(1 + side)
+        rows = pl.ds(HALF - first, HALF)
+        arrivals.append(
+            send(pb.at[1 + side, rows], rsl.at[side, rows], rs_send.at[side, 2], rs_recv.at[side, 2], k)
+        )
+    handshake_3()
+    finish(0)
+    finish(1)
+    compute(PIECES - 1)
     handshake_4()
 
     for yy, cc in mates[:-1]:
@@ -205,29 +193,27 @@
     position = lax.broadcasted_iota(jnp.int32, (SEQ, 1), 0)
     embeds = {}
 
-    def pool(p):
-        for wait in arrivals[p]:
-            wait()
-        for half in range(2):
-            rows = pl.ds(pl.multiple_of(OWN * x + SEQ * half, SEQ), SEQ)
-            there = pl.ds(SEQ * half, SEQ)
-            summed = pb[p, x, there].astype(F32)
-            for k in (0, 2) if p in JOINED else range(NX - 1):
-                summed = summed + rsr[p, k, there].astype(F32)
-            mixed = (xt[p, rows].astype(F32) + summed).astype(BF16).astype(F32)
-            mean = jnp.mean(mixed, axis=1, keepdims=True)
-            centred = mixed - mean
-            variance = jnp.mean(centred * centred, axis=1, keepdims=True)
-            normed = centred * lax.rsqrt(variance + 1e-05) * gain
-            length = len_ref[8 * p + 2 * x + half]
-            kept = jnp.where(position < length, normed, 0.0)
-            pooled = jnp.sum(kept, axis=0, keepdims=True) / length.astype(F32)
-            scale = lax.rsqrt(jnp.mean(pooled * pooled, axis=1, keepdims=True) + 1e-05)
-            embeds[p, half] = pooled * scale
-
-    for p in (0, 3, 1, 2):
-        pool(p)
-    embed = jnp.concatenate([embeds[p, half] for p in range(PIECES) for half in range(2)], axis=0)
+    def pool(label):
+        rows = pl.ds(SEQ * label, SEQ)
+        summed = pb[PIECES - 1, rows, :].astype(F32)
+        for side in range(2):
+            summed = summed + rsl[side, rows, :].astype(F32)
+        mixed = (xt[rows, :].astype(F32) + summed).astype(BF16).astype(F32)
+        mean = jnp.mean(mixed, axis=1, keepdims=True)
+        centred = mixed - mean
+        variance = jnp.mean(centred * centred, axis=1, keepdims=True)
+        normed = centred * lax.rsqrt(variance + 1e-05) * gain
+        length = len_ref[8 * x + label]
+        kept = jnp.where(position < length, normed, 0.0)
+        pooled = jnp.sum(kept, axis=0, keepdims=True) / length.astype(F32)
+        embeds[label] = pooled * lax.rsqrt(jnp.mean(pooled * pooled, axis=1, keepdims=True) + 1e-05)
+
+    for copies, group in ((arrivals[:4], (0, 1, 4, 5)), (arrivals[4:], (2, 3, 6, 7))):
+        for copy in copies:
+            copy.wait_recv()
+        for label in group:
+            pool(label)
+    embed = jnp.concatenate([embeds[label] for label in range(8)], axis=0)
     zero = jnp.zeros((8, PAD - SHARE), F32)
     for s in range(NX):
         part = embed[:, SHARE * s : SHARE * (s + 1)]
@@ -283,9 +269,7 @@
     whole = [
         jnp.concatenate([wide[s, b].astype(F32)[:, :SHARE] for b in range(NX)], axis=1) for s in range(NX)
     ]
-    embed_out[...] = jnp.concatenate(
-        [whole[s][2 * p : 2 * p + 2] for p in range(PIECES) for s in range(NX)], axis=0
-    ).astype(BF16)
+    embed_out[...] = jnp.concatenate(whole, axis=0).astype(BF16)
 
     got = zrecv.at[pl.ds(0, nz - 1)]
     got = remote(got, got, z1_send, z1_recv, **right)
@@ -372,12 +356,12 @@
             vmem((1, LAB), jnp.int32),
             vmem((1, LEAF), jnp.int32),
             vmem((PIECES, NX, SHARE, TOK), BF16),
-            vmem((PIECES, TOK, WIDE), BF16),
+            vmem((TOK, WIDE), BF16),
             vmem((WIDE, WIDE), BF16),
             vmem((WIDE, WIDE), BF16),
-            vmem((PIECES, NX, OWN, WIDE), BF16),
-            vmem((PIECES, NX - 1, OWN, WIDE), BF16),
-            vmem((len(JOINED), OWN, WIDE), BF16),
+            vmem((PIECES, TOK, WIDE), BF16),
+            vmem((2, TOK, WIDE), BF16),
+            vmem((2, 2, PART, WIDE), BF16),
             vmem((8, 128), jnp.int32),
             vmem((plane, 8, 128), jnp.int32),
             vmem((nz * LEAF, plane * LAB), F32),
@@ -394,8 +378,7 @@
             vmem((nz, PAR, PAD), F32),
             regular, regular, regular, regular((3,)),
             dma((PIECES + 6,)),
-            dma((PIECES, NX)), dma((PIECES, NX)), dma((PIECES, NX)), dma((PIECES, NX)),
-            dma((3, NX)), dma((3, NX)), dma((3, NX)), dma((3, NX)),
+            dma((PIECES, NX)), dma((PIECES, NX)), dma((2, 3)), dma((2, 3)), dma((2, 2)), dma((2, 2)),
             dma(()), dma(()), dma(()), dma(()),
             dma((NX,)), dma((NX,)),
             dma(()), dma(()), dma(()), dma(()), dma(()), dma(()), dma(()), dma(()),

time: 57.5 us -> 55.9 us (0.972)
  Pallas kernels: 56.7 us -> 55.1 us
    pallas_call x1, Pallas kernels: 56.1 us -> 54.5 us  [local(): pl.pallas_call(functools.partial(kernel, ny, nz, nc), out_shape=tuple((vm...]
where the time goes in v5:
time: 55.9 us; the launch traced here: 55.8 us
  Pallas kernels  55.1 us (99%)
  between operations  0.64 us (1%)
    pallas_call x1, Pallas kernels, local(): pl.pallas_call(functools.partial(kernel, ny, nz, nc), out_shape=tuple((vm...  54.5 us

profile of v5, /device:TPU:1, one launch (start us, length us, event | category | flops | bytes accessed | tf_op | source)
XLA Modules:
  0.0 55.8 jit_solution(7749946463306968955)
XLA Ops:
  0.6 54.5 %shard_map.94 = (bf16[32,768]{1,0:T(8,128)(2,1)S(1)}, f32[8,192]{1,0:T(8,128)S(1)}, f32[2,192]{1,0:T(2,128)S(1)}) custom-call(s32[32]{0:T(128)} %length_in.1, bf16[192,512]{1,0:T(8,128)(2,1)} %bitcast.3, bf16[768,768]{1,0:T(8,128)(2,1)} %w_up.1, bf16[768,768]{1,0:T(8,128)(2,1)} %w_down.1, f32[768]{0:T(1024)} %gain_in.1, s32[1,32]{1,0:T(1,128)} %bitcast.4, ...), custom_call_target="tpu_custom_call" | custom-call | tf_op jit(solution)/shard_map/pallas_call | solution.py:348
  55.1 0.6 %shard_map.95 = (bf16[32,768]{1,0:T(8,128)(2,1)}, f32[8,192]{1,0:T(8,128)}, f32[2,192]{1,0:T(2,128)}) custom-call(bf16[32,768]{1,0:T(8,128)(2,1)S(1)} %get-tuple-element.6.refs_0_, f32[8,192]{1,0:T(8,128)S(1)} %get-tuple-element.7.refs_1_, f32[2,192]{1,0:T(2,128)S(1)} %get-tuple-element.8.refs_2_), custom_call_target="tpu_custom_call" | custom-call | tf_op jit(solution)/shard_map/pallas_call | solution.py:396

commit v6 on v5

--- a/solution.py
+++ b/solution.py
@@ -39,7 +39,7 @@
     len_ref, gain_ref, leaf_ref, parent_ref, xg, xt, upv, downv, pb, rsl, near, table, tables, pick_leaf, pick_parent, blocks, lab, wide,
     zbuf, zrecv, sbuf, srecv, qrecv, pbuf, precv,
     near_y, far_y, other_c, hops_z,
-    local_sem, ag_send, ag_recv, rs_send, rs_recv, d2_send, d2_recv,
+    local_sem, ag_send, ag_recv, f_send, f_recv, rs_send, rs_recv, d2_send, d2_recv,
     t_send, t_recv, s1_send, s1_recv, e_send, e_recv, z1_send, z1_recv,
     s2_send, s2_recv, q_send, q_recv, z2_send, z2_recv,
 ):
@@ -91,7 +91,7 @@
     ag = {}
 
     def gather(p):
-        for k in (2, 1, 3):
+        for k in (1, 3, 2) if p == 0 else (1, 3):
             to = lax.rem(x + k, NX)
             copy = remote(piece_of(to, p), xg.at[p, x], ag_send.at[p, k], ag_recv.at[p, k], **{AX: to})
             copy.start()
@@ -100,6 +100,34 @@
 
     for p in range(PIECES - 1):
         gather(p)
+    passed = []
+
+    def pass_on(n, p, k, step, rows):
+        ag[p, k].wait_recv()
+        source, to = lax.rem(x + NX - k, NX), {AX: lax.rem(x + k, NX)}
+        passed.append(
+            remote(xg.at[p, source, rows], xg.at[step, source, rows], f_send.at[n], f_recv.at[n], **to)
+        )
+        passed[n].start()
+        drain.append(passed[n].wait_send)
+
+    def collect(p):
+        every, half = pl.ds(0, SHARE), SHARE // 2
+        if p == 0:
+            pass_on(0, 0, 1, 1, every)
+            pass_on(1, 0, 3, 2, every)
+            ag[0, 2].wait_recv()
+        elif p == 1:
+            pass_on(2, 1, 1, 3, pl.ds(0, half))
+            ag[1, 3].wait_recv()
+            passed[0].wait_recv()
+        elif p == 2:
+            pass_on(3, 2, 3, 3, pl.ds(half, half))
+            ag[2, 1].wait_recv()
+            passed[1].wait_recv()
+        else:
+            for copy in (ag[3, 1], ag[3, 3], passed[2], passed[3]):
+                copy.wait_recv()
 
     around(AY, y, ny, 1, near_y)
     steps = [s for s in (1, 2, 4) if 2 * s <= nz // 2]
@@ -134,8 +162,7 @@
     table[1:2, 0:LEAF] = parent_ref[...]
 
     def compute(p):
-        for k in (2, 1, 3):
-            ag[p, k].wait_recv()
+        collect(p)
         features = xg[p].reshape(WIDE, TOK).T
         if p == PIECES - 1:
             xt[...] = features
@@ -378,7 +405,7 @@
             vmem((nz, PAR, PAD), F32),
             regular, regular, regular, regular((3,)),
             dma((PIECES + 6,)),
-            dma((PIECES, NX)), dma((PIECES, NX)), dma((2, 3)), dma((2, 3)), dma((2, 2)), dma((2, 2)),
+            dma((PIECES, NX)), dma((PIECES, NX)), dma((4,)), dma((4,)), dma((2, 3)), dma((2, 3)), dma((2, 2)), dma((2, 2)),
             dma(()), dma(()), dma(()), dma(()),
             dma((NX,)), dma((NX,)),
             dma(()), dma(()), dma(()), dma(()), dma(()), dma(()), dma(()), dma(()),

time: 55.9 us -> 54.8 us (0.980)
  Pallas kernels: 55.1 us -> 54 us
    pallas_call x1, Pallas kernels: 54.5 us -> 53.4 us  [local(): pl.pallas_call(functools.partial(kernel, ny, nz, nc), out_shape=tuple((vm...]
where the time goes in v6:
time: 54.8 us; the launch traced here: 54.7 us
  Pallas kernels  54 us (99%)
  between operations  0.64 us (1%)
    pallas_call x1, Pallas kernels, local(): pl.pallas_call(functools.partial(kernel, ny, nz, nc), out_shape=tuple((vm...  53.4 us

profile of v6, /device:TPU:1, one launch (start us, length us, event | category | flops | bytes accessed | tf_op | source)
XLA Modules:
  0.0 54.7 jit_solution(2503943814590415523)
XLA Ops:
  0.6 53.4 %shard_map.94 = (bf16[32,768]{1,0:T(8,128)(2,1)S(1)}, f32[8,192]{1,0:T(8,128)S(1)}, f32[2,192]{1,0:T(2,128)S(1)}) custom-call(s32[32]{0:T(128)} %length_in.1, bf16[192,512]{1,0:T(8,128)(2,1)} %bitcast.3, bf16[768,768]{1,0:T(8,128)(2,1)} %w_up.1, bf16[768,768]{1,0:T(8,128)(2,1)} %w_down.1, f32[768]{0:T(1024)} %gain_in.1, s32[1,32]{1,0:T(1,128)} %bitcast.4, ...), custom_call_target="tpu_custom_call" | custom-call | tf_op jit(solution)/shard_map/pallas_call | solution.py:375
  54.0 0.6 %shard_map.95 = (bf16[32,768]{1,0:T(8,128)(2,1)}, f32[8,192]{1,0:T(8,128)}, f32[2,192]{1,0:T(2,128)}) custom-call(bf16[32,768]{1,0:T(8,128)(2,1)S(1)} %get-tuple-element.6.refs_0_, f32[8,192]{1,0:T(8,128)S(1)} %get-tuple-element.7.refs_1_, f32[2,192]{1,0:T(2,128)S(1)} %get-tuple-element.8.refs_2_), custom_call_target="tpu_custom_call" | custom-call | tf_op jit(solution)/shard_map/pallas_call | solution.py:423

commit v7 on v6

--- a/solution.py
+++ b/solution.py
@@ -37,7 +37,7 @@
     length_in, hidden, w_up, w_down, gain_in, leaf_in, parent_in,
     embed_out, centers_out, sums_out,
     len_ref, gain_ref, leaf_ref, parent_ref, xg, xt, upv, downv, pb, rsl, near, table, tables, pick_leaf, pick_parent, blocks, lab, wide,
-    zbuf, zrecv, sbuf, srecv, qrecv, pbuf, precv,
+    zbuf, zrecv, sbuf, srecv, sqrow, qrecv, pbuf, precv,
     near_y, far_y, other_c, hops_z,
     local_sem, ag_send, ag_recv, f_send, f_recv, rs_send, rs_recv, d2_send, d2_recv,
     t_send, t_recv, s1_send, s1_recv, e_send, e_recv, z1_send, z1_recv,
@@ -116,6 +116,7 @@
         if p == 0:
             pass_on(0, 0, 1, 1, every)
             pass_on(1, 0, 3, 2, every)
+            gather(PIECES - 1)
             ag[0, 2].wait_recv()
         elif p == 1:
             pass_on(2, 1, 1, 3, pl.ds(0, half))
@@ -198,7 +199,6 @@
             joins[side, part] = send(
                 pb.at[0, rows], near.at[side, part], d2_send.at[side, part], d2_recv.at[side, part], k
             )
-    gather(PIECES - 1)
     handshake_2()
     for side, k, first in sides:
         compute(1 + side)
@@ -304,28 +304,30 @@
     got.wait_recv()
     leaf_sum = jnp.sum(zrecv[...].astype(F32), axis=0)
     square = jnp.sum(leaf_sum * leaf_sum, axis=1, keepdims=True)
-    lane = lax.broadcasted_iota(jnp.int32, (LEAF, PAD), 1)
-    sbuf[...] = jnp.where(lane < SHARE, leaf_sum, square)
+    sbuf[...] = leaf_sum
+    diagonal = lax.broadcasted_iota(jnp.int32, (LEAF, 128), 0) == lax.broadcasted_iota(jnp.int32, (LEAF, 128), 1)
+    sqrow[...] = jnp.sum(jnp.where(diagonal, square, 0.0), axis=0, keepdims=True)
 
     for n, (yy, cc) in enumerate(mates):
         for k in x_order:
             to = {AY: yy, AC: cc, AX: lax.rem(x + k, NX)}
-            if k > 0:
-                remote(sbuf.at[:, pl.ds(128, 128)], qrecv.at[x, here], q_send, q_recv, **to).start()
-            elif n < plane - 1:
+            if k > 0 or n < plane - 1:
+                remote(sqrow, qrecv.at[x * plane + here], q_send, q_recv, **to).start()
+            if k == 0 and n < plane - 1:
                 remote(sbuf, srecv.at[here], s2_send, s2_recv, **to).start()
+    qrecv[x * plane + here] = sqrow[...]
     srecv[here] = sbuf[...]
-    qrecv[x] = jnp.zeros_like(qrecv[x])
     got = srecv.at[pl.ds(0, plane - 1)]
     got = remote(got, got, s2_send, s2_recv, **right)
     drain.append(got.wait_send)
     got.wait_recv()
-    got = qrecv.at[pl.ds(0, NX - 1)]
+    got = qrecv.at[pl.ds(0, NX * plane - 1)]
     got = remote(got, got, q_send, q_recv, **right)
     drain.append(got.wait_send)
     got.wait_recv()
     sums = srecv[...]
-    total = sums[:, :, PAD - 1 :] + jnp.sum(qrecv[...], axis=0)[:, :, 127:]
+    rows = jnp.sum(qrecv[...].reshape(NX, plane, 1, 128), axis=0)
+    total = jnp.sum(jnp.where(diagonal[None], rows, 0.0), axis=2, keepdims=True)
     centers = (sums * lax.rsqrt(total / WIDE + 1e-05)).reshape(plane * LEAF, PAD)
     parts = []
     rest = centers
@@ -342,9 +344,10 @@
         remote(pbuf.at[to], precv.at[z], z2_send, z2_recv, **{AZ: to}).start()
     precv[z] = pbuf[z]
     mine = srecv[here]
-    total = mine[:, PAD - 1 :]
-    for s in range(NX):
-        total = total + qrecv[s, here][:, 127:]
+    row = qrecv[here]
+    for s in range(1, NX):
+        row = row + qrecv[s * plane + here]
+    total = jnp.sum(jnp.where(diagonal, row, 0.0), axis=1, keepdims=True)
     centers_out[...] = (mine * lax.rsqrt(total / WIDE + 1e-05))[:, :SHARE]
     got = precv.at[pl.ds(0, nz - 1)]
     got = remote(got, got, z2_send, z2_recv, **right)
@@ -400,7 +403,8 @@
             vmem((nz, LEAF, PAD), BF16),
             vmem((LEAF, PAD), F32),
             vmem((plane, LEAF, PAD), F32),
-            vmem((NX, plane, LEAF, 128), F32),
+            vmem((1, 128), F32),
+            vmem((NX * plane, 1, 128), F32),
             vmem((nz, PAR, PAD), F32),
             vmem((nz, PAR, PAD), F32),
             regular, regular, regular, regular((3,)),

time: 54.8 us -> 54.4 us (level)
  no operation moved by 1% of the time
where the time goes in v7:
time: 54.4 us; the launch traced here: 54.3 us
  Pallas kernels  53.7 us (99%)
  between operations  0.64 us (1%)
    pallas_call x1, Pallas kernels, local(): pl.pallas_call(functools.partial(kernel, ny, nz, nc), out_shape=tuple((vm...  53 us

profile of v7, /device:TPU:1, one launch (start us, length us, event | category | flops | bytes accessed | tf_op | source)
XLA Modules:
  0.0 54.3 jit_solution(13941419654303324743)
XLA Ops:
  0.6 53.0 %shard_map.94 = (bf16[32,768]{1,0:T(8,128)(2,1)S(1)}, f32[8,192]{1,0:T(8,128)S(1)}, f32[2,192]{1,0:T(2,128)S(1)}) custom-call(s32[32]{0:T(128)} %length_in.1, bf16[192,512]{1,0:T(8,128)(2,1)} %bitcast.3, bf16[768,768]{1,0:T(8,128)(2,1)} %w_up.1, bf16[768,768]{1,0:T(8,128)(2,1)} %w_down.1, f32[768]{0:T(1024)} %gain_in.1, s32[1,32]{1,0:T(1,128)} %bitcast.4, ...), custom_call_target="tpu_custom_call" | custom-call | tf_op jit(solution)/shard_map/pallas_call | solution.py:378
  53.7 0.6 %shard_map.95 = (bf16[32,768]{1,0:T(8,128)(2,1)}, f32[8,192]{1,0:T(8,128)}, f32[2,192]{1,0:T(2,128)}) custom-call(bf16[32,768]{1,0:T(8,128)(2,1)S(1)} %get-tuple-element.6.refs_0_, f32[8,192]{1,0:T(8,128)S(1)} %get-tuple-element.7.refs_1_, f32[2,192]{1,0:T(2,128)S(1)} %get-tuple-element.8.refs_2_), custom_call_target="tpu_custom_call" | custom-call | tf_op jit(solution)/shard_map/pallas_call | solution.py:427
